TPU v7x, 512 devices: a whole 4x4x16 slice. The times are simulated.
512 devices in a mesh: section: 8 (over y, core), seq: 64 (over x, z).
Axes of the slice: x: 4, y: 4, z: 16, core: 2. Of those that a mesh axis runs over, the one named last changes fastest.
Arguments:
- slab_rows: bfloat16 [8192, 4096], P('seq'), may hold values from -10 to 10
- filter_taps: bfloat16 [8, 256, 128], P('section', 'seq'), may hold values from -0.5 to 0.5
- skip_weights: bfloat16 [8, 4096], P('section', 'seq'), may hold values from -0.59765625 to 0.59765625
Outputs:
- section_outputs: bfloat16 [8, 8192, 4096], P('section', 'seq')
- tap_hessians: float32 [8, 256, 128, 128], P('section', 'seq')
All inputs are finite; a program needn't handle non-finite values.
Results may differ from a plain program's by a relative error of at most 0.0073.
Values may be sent and summed in bfloat16 or wider, within the bound.
No kernel may reach another device: no remote copies, remote signals or barrier semaphores. Data moves between devices by JAX's collectives and lax.ppermute only.
A program may use at most 64 MiB of HBM per device.

v0:
```python
import jax
import jax.numpy as jnp
from jax import lax
from jax.sharding import PartitionSpec as P

GROUP = 16
TAPS = 128
MICRO = 4


def shifted(value, axis, steps):
    count = lax.axis_size(axis)
    leading, last = (max(0, -steps), min(count, count - steps))
    return lax.ppermute(value, axis, [(source, source + steps) for source in range(leading, last)])


def toeplitz(taps_row):
    out_pos = jnp.arange(TAPS)[:, None]
    in_pos = jnp.arange(2 * TAPS)[None, :]
    lag_index = TAPS + out_pos - in_pos
    active = (lag_index >= 0) & (lag_index < TAPS)
    tap_table = taps_row[:, jnp.clip(lag_index, 0, TAPS - 1)]
    return jnp.where(active[None], tap_table, jnp.zeros_like(tap_table))


def windows(current, earlier):
    nblocks = current.shape[0] // TAPS
    groups_here = current.shape[1] // GROUP
    blocks = current.reshape(nblocks, TAPS, groups_here, GROUP)
    before = jnp.concatenate([earlier.reshape(1, TAPS, groups_here, GROUP), blocks[:-1]], axis=0)
    return jnp.concatenate([before, blocks], axis=1)


def gram_window(window_rows):
    before = window_rows[:, :TAPS]
    present = window_rows[:, TAPS:]
    cur_part = jnp.einsum("nsgc,nrgc->gsr", present, present, preferred_element_type=jnp.float32)
    cross = jnp.einsum("nsgc,nrgc->gsr", before, present, preferred_element_type=jnp.float32)
    first = jnp.einsum("sgc,rgc->gsr", before[0], before[0], preferred_element_type=jnp.float32)
    last = jnp.einsum("sgc,rgc->gsr", present[-1], present[-1], preferred_element_type=jnp.float32)
    prev_part = cur_part - last + first
    top = jnp.concatenate([prev_part, cross], axis=2)
    bottom = jnp.concatenate([jnp.swapaxes(cross, 1, 2), cur_part], axis=2)
    return jnp.concatenate([top, bottom], axis=1)


def diag_prefix(gram_sum):
    running = gram_sum
    size = gram_sum.shape[-1]
    offset = 1
    while offset < size:
        widths = [(0, 0)] * (running.ndim - 2) + [(offset, 0), (offset, 0)]
        running = running + jnp.pad(running, widths)[..., :size, :size]
        offset = offset * 2
    return running


def tap_hessian(gram_sum):
    prefix = diag_prefix(gram_sum)
    return (prefix[..., TAPS:, TAPS:] - prefix[..., :TAPS, :TAPS])[..., ::-1, ::-1]


def per_device(slab_rows, filter_taps, skip_weights):
    section_total = lax.axis_size("section")
    section_index = lax.axis_index("section")
    channels = lax.all_to_all(slab_rows, "seq", split_axis=1, concat_axis=0, tiled=True)
    length, chan_width = channels.shape
    groups_here = chan_width // GROUP
    matrix = toeplitz(filter_taps[0])
    skip_gain = skip_weights[0].astype(jnp.float32)[None, :]
    micro_count = MICRO
    piece_len = length // micro_count

    def advance(step_no, carry):
        received, tail_rows, gram_sum, result = carry
        micro_index = step_no - section_index
        active = (micro_index >= 0) & (micro_index < micro_count)
        micro_clip = jnp.clip(micro_index, 0, micro_count - 1)
        row_start = micro_clip * piece_len
        source_rows = lax.dynamic_slice_in_dim(channels, row_start, piece_len, 0)
        section_in = jnp.where(section_index == 0, source_rows, received)
        earlier = jnp.where(micro_clip == 0, jnp.zeros_like(tail_rows), tail_rows)
        blocks = windows(section_in, earlier)
        filtered = jnp.einsum(
            "gts,nsgc->ntgc", matrix, blocks, preferred_element_type=jnp.float32
        ).reshape(piece_len, chan_width)
        filtered = (filtered + skip_gain * section_in.astype(jnp.float32)).astype(jnp.bfloat16)
        gram_part = gram_window(blocks)
        gram_sum = gram_sum + jnp.where(active, gram_part, jnp.zeros_like(gram_part))
        kept_rows = lax.dynamic_slice_in_dim(result, row_start, piece_len, 0)
        result = lax.dynamic_update_slice_in_dim(
            result, jnp.where(active, filtered, kept_rows), row_start, 0
        )
        tail_rows = jnp.where(active, section_in[piece_len - TAPS :], tail_rows)
        received = shifted(filtered, "section", 1)
        return (received, tail_rows, gram_sum, result)

    initial = (
        jnp.zeros((piece_len, chan_width), jnp.bfloat16),
        jnp.zeros((TAPS, chan_width), jnp.bfloat16),
        jnp.zeros((groups_here, 2 * TAPS, 2 * TAPS), jnp.float32),
        jnp.zeros((length, chan_width), jnp.bfloat16),
    )
    received, tail_rows, gram_sum, result = lax.fori_loop(
        0, section_total + micro_count - 1, advance, initial
    )
    hessians = tap_hessian(gram_sum) * (2.0 / (length * GROUP))
    restored = lax.all_to_all(result, "seq", split_axis=0, concat_axis=1, tiled=True)
    return (restored[None], hessians[None])


def solution(mesh):
    in_specs = (P("seq", None), P("section", "seq", None), P("section", "seq"))
    out_specs = (P("section", "seq", None), P("section", "seq", None, None))
    return jax.shard_map(
        per_device, mesh=mesh, in_specs=in_specs, out_specs=out_specs, check_vma=False
    )
```

profile of v0, /device:TPU:1, one launch (start us, length us, event | category | flops | bytes accessed | tf_op | source)
XLA Modules:
  0.0 334.2 jit_solution(11933325957089993826)
XLA Ops:
  0.6 2.3 copy.45
  2.9 19.2 %all-to-all-start = ((bf16[128,64,64]{0,2,1:T(8,128)(2,1)}), bf16[128,64,64]{0,2,1:T(8,128)(2,1)S(1)}, u32[]{:S(2)}, u32[]{:S(2)}) async-start(bf16[128,64,64]{0,2,1:T(8,128)(2,1)} %bitcast), calls=%async_computation | async-start | bytes 2097152 | tf_op jit(solution)/shard_map/all_to_all | solution.py:66
  22.5 114.2 %gather_fusion = bf16[32768,4]{1,0:T(8,128)(2,1)} fusion(bf16[4,128]{0,1:T(8,128)(2,1)S(1)} %bitcast.101, s32[32768]{0:T(1024)S(1)} %broadcast_clamp_fusion), kind=kCustom, calls=%fused_computation | custom fusion | bytes 655360 | tf_op jit(solution)/shard_map/gather | solution.py:22
  136.7 7.1 %copy.48 = bf16[128,256,4]{1,0,2:T(8,128)(2,1)S(1)} copy(bf16[128,256,4]{2,1,0:T(8,128)(2,1)} %bitcast.109) | data formatting | bytes 524288 | tf_op jit(solution)/shard_map/gather | solution.py:22
  145.8 119.7 %while.21 = (s32[]{:T(128)}, bf16[2048,64]{0,1:T(8,128)(2,1)S(1)}, bf16[128,64]{0,1:T(8,128)(2,1)S(1)}, f32[4,256,256]{1,2,0:T(8,128)S(1)}, bf16[8192,64]{0,1:T(...) while((s32[]{:T(128)}, bf16[2048,64]{0,1:T(8,128)(2,1)S(1)}, ...), condition=%wide.region_1.2_spmd.clone, body=%wide.region_0.1_spmd.clone.sunk | while | flops 142630928 | bytes 14435141 | solution.py:104
  147.4 1.2 convolution_bitcast_fusion.4
  149.1 4.0 %collective-permute-start = (bf16[2048,64]{0,1:T(8,128)(2,1)S(1)}, bf16[2048,64]{0,1:T(8,128)(2,1)S(1)}, u32[]{:S(2)}, u32[]{:S(2)}) collective-permute-start(bf16[2048,64]{0,1:T(8,128)(2,1)S(1)} %get-tuple-element.331), channel_id=1, source_target_pairs={{0,64},{64,128},{128,192},{192,256},{256,320},{320,384},{384,448},... | collective-permute-start | bytes 786440 | tf_op jit(solution)/shard_map/while/body/eval_jaxpr/ppermute | solution.py:14
  154.7 1.8 collective-permute-done
  159.7 4.4 %collective-permute-start = (bf16[2048,64]{0,1:T(8,128)(2,1)S(1)}, bf16[2048,64]{0,1:T(8,128)(2,1)S(1)}, u32[]{:S(2)}, u32[]{:S(2)}) collective-permute-start(bf16[2048,64]{0,1:T(8,128)(2,1)S(1)} %get-tuple-element.331), channel_id=1, source_target_pairs={{0,64},{64,128},{128,192},{192,256},{256,320},{320,384},{384,448},... | collective-permute-start | bytes 786440 | tf_op jit(solution)/shard_map/while/body/eval_jaxpr/ppermute | solution.py:14
  165.6 1.8 collective-permute-done
  170.6 4.4 %collective-permute-start = (bf16[2048,64]{0,1:T(8,128)(2,1)S(1)}, bf16[2048,64]{0,1:T(8,128)(2,1)S(1)}, u32[]{:S(2)}, u32[]{:S(2)}) collective-permute-start(bf16[2048,64]{0,1:T(8,128)(2,1)S(1)} %get-tuple-element.331), channel_id=1, source_target_pairs={{0,64},{64,128},{128,192},{192,256},{256,320},{320,384},{384,448},... | collective-permute-start | bytes 786440 | tf_op jit(solution)/shard_map/while/body/eval_jaxpr/ppermute | solution.py:14
  176.5 1.8 collective-permute-done
  181.5 4.4 %collective-permute-start = (bf16[2048,64]{0,1:T(8,128)(2,1)S(1)}, bf16[2048,64]{0,1:T(8,128)(2,1)S(1)}, u32[]{:S(2)}, u32[]{:S(2)}) collective-permute-start(bf16[2048,64]{0,1:T(8,128)(2,1)S(1)} %get-tuple-element.331), channel_id=1, source_target_pairs={{0,64},{64,128},{128,192},{192,256},{256,320},{320,384},{384,448},... | collective-permute-start | bytes 786440 | tf_op jit(solution)/shard_map/while/body/eval_jaxpr/ppermute | solution.py:14
  187.4 1.8 collective-permute-done
  192.4 4.4 %collective-permute-start = (bf16[2048,64]{0,1:T(8,128)(2,1)S(1)}, bf16[2048,64]{0,1:T(8,128)(2,1)S(1)}, u32[]{:S(2)}, u32[]{:S(2)}) collective-permute-start(bf16[2048,64]{0,1:T(8,128)(2,1)S(1)} %get-tuple-element.331), channel_id=1, source_target_pairs={{0,64},{64,128},{128,192},{192,256},{256,320},{320,384},{384,448},... | collective-permute-start | bytes 786440 | tf_op jit(solution)/shard_map/while/body/eval_jaxpr/ppermute | solution.py:14
  198.3 1.8 collective-permute-done
  203.3 4.4 %collective-permute-start = (bf16[2048,64]{0,1:T(8,128)(2,1)S(1)}, bf16[2048,64]{0,1:T(8,128)(2,1)S(1)}, u32[]{:S(2)}, u32[]{:S(2)}) collective-permute-start(bf16[2048,64]{0,1:T(8,128)(2,1)S(1)} %get-tuple-element.331), channel_id=1, source_target_pairs={{0,64},{64,128},{128,192},{192,256},{256,320},{320,384},{384,448},... | collective-permute-start | bytes 786440 | tf_op jit(solution)/shard_map/while/body/eval_jaxpr/ppermute | solution.py:14
  209.3 1.8 collective-permute-done
  214.2 4.4 %collective-permute-start = (bf16[2048,64]{0,1:T(8,128)(2,1)S(1)}, bf16[2048,64]{0,1:T(8,128)(2,1)S(1)}, u32[]{:S(2)}, u32[]{:S(2)}) collective-permute-start(bf16[2048,64]{0,1:T(8,128)(2,1)S(1)} %get-tuple-element.331), channel_id=1, source_target_pairs={{0,64},{64,128},{128,192},{192,256},{256,320},{320,384},{384,448},... | collective-permute-start | bytes 786440 | tf_op jit(solution)/shard_map/while/body/eval_jaxpr/ppermute | solution.py:14
  220.2 1.8 collective-permute-done
  225.1 4.4 %collective-permute-start = (bf16[2048,64]{0,1:T(8,128)(2,1)S(1)}, bf16[2048,64]{0,1:T(8,128)(2,1)S(1)}, u32[]{:S(2)}, u32[]{:S(2)}) collective-permute-start(bf16[2048,64]{0,1:T(8,128)(2,1)S(1)} %get-tuple-element.331), channel_id=1, source_target_pairs={{0,64},{64,128},{128,192},{192,256},{256,320},{320,384},{384,448},... | collective-permute-start | bytes 786440 | tf_op jit(solution)/shard_map/while/body/eval_jaxpr/ppermute | solution.py:14
  231.1 1.8 collective-permute-done
  236.1 4.4 %collective-permute-start = (bf16[2048,64]{0,1:T(8,128)(2,1)S(1)}, bf16[2048,64]{0,1:T(8,128)(2,1)S(1)}, u32[]{:S(2)}, u32[]{:S(2)}) collective-permute-start(bf16[2048,64]{0,1:T(8,128)(2,1)S(1)} %get-tuple-element.331), channel_id=1, source_target_pairs={{0,64},{64,128},{128,192},{192,256},{256,320},{320,384},{384,448},... | collective-permute-start | bytes 786440 | tf_op jit(solution)/shard_map/while/body/eval_jaxpr/ppermute | solution.py:14
  242.0 1.8 collective-permute-done
  247.0 4.4 %collective-permute-start = (bf16[2048,64]{0,1:T(8,128)(2,1)S(1)}, bf16[2048,64]{0,1:T(8,128)(2,1)S(1)}, u32[]{:S(2)}, u32[]{:S(2)}) collective-permute-start(bf16[2048,64]{0,1:T(8,128)(2,1)S(1)} %get-tuple-element.331), channel_id=1, source_target_pairs={{0,64},{64,128},{128,192},{192,256},{256,320},{320,384},{384,448},... | collective-permute-start | bytes 786440 | tf_op jit(solution)/shard_map/while/body/eval_jaxpr/ppermute | solution.py:14
  252.9 1.8 collective-permute-done
  257.9 4.4 %collective-permute-start = (bf16[2048,64]{0,1:T(8,128)(2,1)S(1)}, bf16[2048,64]{0,1:T(8,128)(2,1)S(1)}, u32[]{:S(2)}, u32[]{:S(2)}) collective-permute-start(bf16[2048,64]{0,1:T(8,128)(2,1)S(1)} %get-tuple-element.331), channel_id=1, source_target_pairs={{0,64},{64,128},{128,192},{192,256},{256,320},{320,384},{384,448},... | collective-permute-start | bytes 786440 | tf_op jit(solution)/shard_map/while/body/eval_jaxpr/ppermute | solution.py:14
  263.8 1.8 collective-permute-done
  265.6 1.3 copy_bitcast_fusion.1
  266.8 14.9 %all-to-all-start.1 = ((bf16[64,128,64]{1,2,0:T(8,128)(2,1)}), bf16[64,128,64]{1,2,0:T(8,128)(2,1)S(1)}, u32[]{:S(2)}, u32[]{:S(2)}) async-start(bf16[64,128,64]{1,2,0:T(8,128)(2,1)} %copy_bitcast_fusion.1), calls=%async_computation.1 | async-start | bytes 2097152 | tf_op jit(solution)/shard_map/all_to_all | solution.py:108
  285.5 47.3 %all-to-all-done.1 = bf16[64,128,64]{1,2,0:T(8,128)(2,1)S(1)} async-done(((bf16[64,128,64]{1,2,0:T(8,128)(2,1)}), bf16[64,128,64]{1,2,0:T(8,128)(2,1)S(1)}, u32[]{:S(2)}, u32[]{:S(2)}) %all-to-all-start.1) | async-done | bytes 1048608 | tf_op jit(solution)/shard_map/all_to_all | solution.py:108
  332.9 1.3 copy.52
  (205 shorter events, 56.2 us)
Async XLA Ops:
  2.9 19.5 %copy-start = (bf16[1,4,128]{2,1,0:T(4,128)(2,1)S(1)}, bf16[1,4,128]{2,1,0:T(4,128)(2,1)}, u32[]{:S(2)}) copy-start(bf16[1,4,128]{2,1,0:T(4,128)(2,1)} %param.6) | copy-start | bytes 3076
  2.9 141.7 %all-to-all-start = ((bf16[128,64,64]{0,2,1:T(8,128)(2,1)}), bf16[128,64,64]{0,2,1:T(8,128)(2,1)S(1)}, u32[]{:S(2)}, u32[]{:S(2)}) async-start(bf16[128,64,64]{0,2,1:T(8,128)(2,1)} %bitcast), calls=%async_computation | async-start | bytes 2097152 | tf_op jit(solution)/shard_map/all_to_all | solution.py:66
  136.7 7.1 %copy-start.1 = (bf16[1,64]{1,0:T(2,128)(2,1)S(1)}, bf16[1,64]{1,0:T(2,128)(2,1)}, u32[]{:S(2)}) copy-start(bf16[1,64]{1,0:T(2,128)(2,1)} %param.7) | copy-start | bytes 388
  149.1 7.3 %collective-permute-start = (bf16[2048,64]{0,1:T(8,128)(2,1)S(1)}, bf16[2048,64]{0,1:T(8,128)(2,1)S(1)}, u32[]{:S(2)}, u32[]{:S(2)}) collective-permute-start(bf16[2048,64]{0,1:T(8,128)(2,1)S(1)} %get-tuple-element.331), channel_id=1, source_target_pairs={{0,64},{64,128},{128,192},{192,256},{256,320},{320,384},{384,448},... | collective-permute-start | bytes 786440 | tf_op jit(solution)/shard_map/while/body/eval_jaxpr/ppermute | solution.py:14
  159.7 7.7 %collective-permute-start = (bf16[2048,64]{0,1:T(8,128)(2,1)S(1)}, bf16[2048,64]{0,1:T(8,128)(2,1)S(1)}, u32[]{:S(2)}, u32[]{:S(2)}) collective-permute-start(bf16[2048,64]{0,1:T(8,128)(2,1)S(1)} %get-tuple-element.331), channel_id=1, source_target_pairs={{0,64},{64,128},{128,192},{192,256},{256,320},{320,384},{384,448},... | collective-permute-start | bytes 786440 | tf_op jit(solution)/shard_map/while/body/eval_jaxpr/ppermute | solution.py:14
  170.6 7.7 %collective-permute-start = (bf16[2048,64]{0,1:T(8,128)(2,1)S(1)}, bf16[2048,64]{0,1:T(8,128)(2,1)S(1)}, u32[]{:S(2)}, u32[]{:S(2)}) collective-permute-start(bf16[2048,64]{0,1:T(8,128)(2,1)S(1)} %get-tuple-element.331), channel_id=1, source_target_pairs={{0,64},{64,128},{128,192},{192,256},{256,320},{320,384},{384,448},... | collective-permute-start | bytes 786440 | tf_op jit(solution)/shard_map/while/body/eval_jaxpr/ppermute | solution.py:14
  181.5 7.7 %collective-permute-start = (bf16[2048,64]{0,1:T(8,128)(2,1)S(1)}, bf16[2048,64]{0,1:T(8,128)(2,1)S(1)}, u32[]{:S(2)}, u32[]{:S(2)}) collective-permute-start(bf16[2048,64]{0,1:T(8,128)(2,1)S(1)} %get-tuple-element.331), channel_id=1, source_target_pairs={{0,64},{64,128},{128,192},{192,256},{256,320},{320,384},{384,448},... | collective-permute-start | bytes 786440 | tf_op jit(solution)/shard_map/while/body/eval_jaxpr/ppermute | solution.py:14
  192.4 7.7 %collective-permute-start = (bf16[2048,64]{0,1:T(8,128)(2,1)S(1)}, bf16[2048,64]{0,1:T(8,128)(2,1)S(1)}, u32[]{:S(2)}, u32[]{:S(2)}) collective-permute-start(bf16[2048,64]{0,1:T(8,128)(2,1)S(1)} %get-tuple-element.331), channel_id=1, source_target_pairs={{0,64},{64,128},{128,192},{192,256},{256,320},{320,384},{384,448},... | collective-permute-start | bytes 786440 | tf_op jit(solution)/shard_map/while/body/eval_jaxpr/ppermute | solution.py:14
  203.3 7.7 %collective-permute-start = (bf16[2048,64]{0,1:T(8,128)(2,1)S(1)}, bf16[2048,64]{0,1:T(8,128)(2,1)S(1)}, u32[]{:S(2)}, u32[]{:S(2)}) collective-permute-start(bf16[2048,64]{0,1:T(8,128)(2,1)S(1)} %get-tuple-element.331), channel_id=1, source_target_pairs={{0,64},{64,128},{128,192},{192,256},{256,320},{320,384},{384,448},... | collective-permute-start | bytes 786440 | tf_op jit(solution)/shard_map/while/body/eval_jaxpr/ppermute | solution.py:14
  214.2 7.7 %collective-permute-start = (bf16[2048,64]{0,1:T(8,128)(2,1)S(1)}, bf16[2048,64]{0,1:T(8,128)(2,1)S(1)}, u32[]{:S(2)}, u32[]{:S(2)}) collective-permute-start(bf16[2048,64]{0,1:T(8,128)(2,1)S(1)} %get-tuple-element.331), channel_id=1, source_target_pairs={{0,64},{64,128},{128,192},{192,256},{256,320},{320,384},{384,448},... | collective-permute-start | bytes 786440 | tf_op jit(solution)/shard_map/while/body/eval_jaxpr/ppermute | solution.py:14
  225.1 7.7 %collective-permute-start = (bf16[2048,64]{0,1:T(8,128)(2,1)S(1)}, bf16[2048,64]{0,1:T(8,128)(2,1)S(1)}, u32[]{:S(2)}, u32[]{:S(2)}) collective-permute-start(bf16[2048,64]{0,1:T(8,128)(2,1)S(1)} %get-tuple-element.331), channel_id=1, source_target_pairs={{0,64},{64,128},{128,192},{192,256},{256,320},{320,384},{384,448},... | collective-permute-start | bytes 786440 | tf_op jit(solution)/shard_map/while/body/eval_jaxpr/ppermute | solution.py:14
  236.1 7.7 %collective-permute-start = (bf16[2048,64]{0,1:T(8,128)(2,1)S(1)}, bf16[2048,64]{0,1:T(8,128)(2,1)S(1)}, u32[]{:S(2)}, u32[]{:S(2)}) collective-permute-start(bf16[2048,64]{0,1:T(8,128)(2,1)S(1)} %get-tuple-element.331), channel_id=1, source_target_pairs={{0,64},{64,128},{128,192},{192,256},{256,320},{320,384},{384,448},... | collective-permute-start | bytes 786440 | tf_op jit(solution)/shard_map/while/body/eval_jaxpr/ppermute | solution.py:14
  247.0 7.7 %collective-permute-start = (bf16[2048,64]{0,1:T(8,128)(2,1)S(1)}, bf16[2048,64]{0,1:T(8,128)(2,1)S(1)}, u32[]{:S(2)}, u32[]{:S(2)}) collective-permute-start(bf16[2048,64]{0,1:T(8,128)(2,1)S(1)} %get-tuple-element.331), channel_id=1, source_target_pairs={{0,64},{64,128},{128,192},{192,256},{256,320},{320,384},{384,448},... | collective-permute-start | bytes 786440 | tf_op jit(solution)/shard_map/while/body/eval_jaxpr/ppermute | solution.py:14
  257.9 7.7 %collective-permute-start = (bf16[2048,64]{0,1:T(8,128)(2,1)S(1)}, bf16[2048,64]{0,1:T(8,128)(2,1)S(1)}, u32[]{:S(2)}, u32[]{:S(2)}) collective-permute-start(bf16[2048,64]{0,1:T(8,128)(2,1)S(1)} %get-tuple-element.331), channel_id=1, source_target_pairs={{0,64},{64,128},{128,192},{192,256},{256,320},{320,384},{384,448},... | collective-permute-start | bytes 786440 | tf_op jit(solution)/shard_map/while/body/eval_jaxpr/ppermute | solution.py:14
  266.8 66.0 %all-to-all-start.1 = ((bf16[64,128,64]{1,2,0:T(8,128)(2,1)}), bf16[64,128,64]{1,2,0:T(8,128)(2,1)S(1)}, u32[]{:S(2)}, u32[]{:S(2)}) async-start(bf16[64,128,64]{1,2,0:T(8,128)(2,1)} %copy_bitcast_fusion.1), calls=%async_computation.1 | async-start | bytes 2097152 | tf_op jit(solution)/shard_map/all_to_all | solution.py:108
where the time goes:
time: 338 us; the launch traced here: 334 us
  local copies, waits for them, and re-layouts  136 us (40%)
  starting transfers between devices  82 us (24%)
  waiting for transfers between devices  66.6 us (20%)
  matrix products  24.9 us (7%)
  other arithmetic  22.6 us (7%)
    gather x2, local copies, waits for them, and re-layouts, toeplitz(): tap_table = taps_row[:, jnp.clip(lag_index, 0, TAPS - 1)]  121 us
    ppermute x11, starting transfers between devices, shifted(): lax.ppermute(value, axis, [(source, source + steps) for source in range(l...  47.9 us
    all_to_all x1, waiting for transfers between devices, per_device(): lax.all_to_all(result, 'seq', split_axis=0, concat_axis=1, tiled=True)  47.3 us
    ppermute x11, waiting for transfers between devices, shifted(): lax.ppermute(value, axis, [(source, source + steps) for source in range(l...  19.3 us
    all_to_all x1, starting transfers between devices, per_device(): lax.all_to_all(slab_rows, 'seq', split_axis=1, concat_axis=0, tiled=True)  19.2 us
    all_to_all x1, starting transfers between devices, per_device(): lax.all_to_all(result, 'seq', split_axis=0, concat_axis=1, tiled=True)  14.9 us
    dot_general x11, matrix products, advance(): jnp.einsum('gts,nsgc->ntgc', matrix, blocks, preferred_element_type=jnp.f...  13.7 us
    select_n x11, other arithmetic, advance(): section_in = jnp.where(section_index == 0, source_rows, received)  11.2 us
  transfers between devices with their start and end apart: 13, of which 12 were waited for; matrix products, arithmetic and copies ran while one was open for 43% of the time, Pallas kernels for 0%

commit v1 on v0

v1 whole, which is shorter than its diff:
```python
import functools

import jax
import jax.numpy as jnp
from jax import lax
from jax.experimental import pallas as pl
from jax.experimental.pallas import tpu as pltpu
from jax.sharding import PartitionSpec as P

GROUP = 16
TAPS = 128
HALF = 8
EDGE = 2 * HALF
INFO = 2 * EDGE
CHUNK = 1024

VMEM = pltpu.VMEM
SMEM = pltpu.SMEM


def pick_kernel(sec_ref, slab_ref, out_ref):
    sec = sec_ref[0]
    width = 256
    rows = width // 8
    out_row = lax.broadcasted_iota(jnp.int32, (rows, width), 0)
    lane = lax.broadcasted_iota(jnp.int32, (rows, width), 1)
    wanted = (out_row // HALF) * 64 + sec * HALF + out_row % HALF
    chosen = jnp.where(lane == wanted, 1.0, 0.0).astype(jnp.bfloat16)
    for piece in range(CHUNK // width):
        part = lax.dot_general(
            chosen,
            slab_ref[:, piece * width : (piece + 1) * width],
            (((1,), (1,)), ((), ())),
            preferred_element_type=jnp.float32,
        )
        out_ref[piece * rows : (piece + 1) * rows, :] = part.astype(jnp.bfloat16)


def pick(sec, slab_rows):
    length, width = slab_rows.shape
    return pl.pallas_call(
        pick_kernel,
        grid_spec=pltpu.PrefetchScalarGridSpec(
            num_scalar_prefetch=1,
            grid=(width // CHUNK,),
            in_specs=[pl.BlockSpec((length, CHUNK), lambda i, s: (0, i))],
            out_specs=pl.BlockSpec((CHUNK // 8, length), lambda i, s: (i, 0)),
        ),
        out_shape=jax.ShapeDtypeStruct((width // 8, length), jnp.bfloat16),
        name="pick",
    )(sec, slab_rows)


def chain_kernel(sec_ref, x_ref, par_ref, y_ref, info_ref, state, par):
    step = pl.program_id(0)
    sec = sec_ref[0]
    rows = state.shape[0]

    @pl.when(step == 0)
    def _():
        state[...] = x_ref[...].astype(jnp.float32)
        par[...] = par_ref[...].astype(jnp.float32)

    slot = step ^ sec
    taps_row = par[pl.ds(slot * 8 + sec // 2, 1), :]
    skip_row = par[pl.ds(slot * 8 + 4, 1), :]
    spread = jnp.concatenate([taps_row, jnp.zeros_like(taps_row)], axis=1)
    spread = jnp.broadcast_to(spread, (TAPS, 2 * TAPS))
    band = pltpu.roll(spread, 0, 1, stride=1, stride_axis=0).astype(jnp.bfloat16)
    lane = lax.broadcasted_iota(jnp.int32, (HALF, TAPS), 1)
    chan = lax.broadcasted_iota(jnp.int32, (HALF, TAPS), 0)
    own = jnp.where(lane == sec * HALF + chan, jnp.broadcast_to(skip_row, (HALF, TAPS)), 0.0)
    gain = jnp.broadcast_to(jnp.sum(own, axis=1, keepdims=True), (HALF, TAPS))

    current = state[...]
    current_b = current.astype(jnp.bfloat16)
    both = jnp.dot(current_b, band, preferred_element_type=jnp.float32)
    blank = jnp.zeros((HALF, TAPS), jnp.float32)
    carried = jnp.concatenate([blank, both[: rows - HALF, TAPS:]], axis=0)
    direct = (current.reshape(rows // HALF, HALF, TAPS) * gain[None]).reshape(rows, TAPS)
    filtered = (both[:, :TAPS] + carried + direct).astype(jnp.bfloat16)
    y_ref[0] = filtered
    state[...] = filtered.astype(jnp.float32)

    body = jnp.concatenate([current[: rows - HALF], blank], axis=0)
    after = jnp.concatenate([body[HALF:], blank], axis=0)
    pair = jnp.concatenate([body, after], axis=1).astype(jnp.bfloat16)
    gram = lax.dot_general(
        current_b, pair, (((0,), (0,)), ((), ())), preferred_element_type=jnp.float32
    )
    size = TAPS
    while size > 8:
        size = size // 2
        gram = gram[:size] + pltpu.roll(gram[size:], 2 * TAPS - size, 1)
    row = lax.broadcasted_iota(jnp.int32, gram.shape, 0)
    for bit in (4, 2, 1):
        gram = jnp.where((row & bit) != 0, pltpu.roll(gram, 2 * TAPS - bit, 1), gram)
    lags = jnp.sum(gram, axis=0, keepdims=True)[:, :TAPS]
    high = lags.astype(jnp.bfloat16).astype(jnp.float32)
    middle = (lags - high).astype(jnp.bfloat16).astype(jnp.float32)
    low = lags - high - middle
    info_row = lax.broadcasted_iota(jnp.int32, (INFO - EDGE, TAPS), 0)
    packed = jnp.where(
        info_row == 0, high, jnp.where(info_row == 1, middle, jnp.where(info_row == 2, low, 0.0))
    )
    info = jnp.concatenate([current[rows - EDGE :], packed], axis=0)
    info_ref[slot] = info.astype(jnp.bfloat16)


def chain(sec, rows_in, params, sections):
    rows = rows_in.shape[0]
    return pl.pallas_call(
        chain_kernel,
        grid_spec=pltpu.PrefetchScalarGridSpec(
            num_scalar_prefetch=1,
            grid=(sections,),
            in_specs=[
                pl.BlockSpec((rows, TAPS), lambda i, s: (0, 0)),
                pl.BlockSpec(params.shape, lambda i, s: (0, 0)),
            ],
            out_specs=[
                pl.BlockSpec((1, rows, TAPS), lambda i, s: (i, 0, 0)),
                pl.BlockSpec((sections, INFO, TAPS), lambda i, s: (0, 0, 0)),
            ],
            scratch_shapes=[VMEM((rows, TAPS), jnp.float32), VMEM(params.shape, jnp.float32)],
        ),
        out_shape=[
            jax.ShapeDtypeStruct((sections, rows, TAPS), jnp.bfloat16),
            jax.ShapeDtypeStruct((sections, INFO, TAPS), jnp.bfloat16),
        ],
        name="chain",
    )(sec, rows_in, params)


def place_kernel(x_ref, out_ref):
    quads = x_ref.shape[1]
    row = lax.broadcasted_iota(jnp.int32, (TAPS, TAPS), 0)
    col = lax.broadcasted_iota(jnp.int32, (TAPS, TAPS), 1)
    same = jnp.where(row == col, 1.0, 0.0).astype(jnp.bfloat16)
    for pair in range(quads // 2):
        parts = [x_ref[r, 2 * pair + half] for half in range(2) for r in range(8)]
        tile = jnp.concatenate(parts, axis=0)
        turned = lax.dot_general(
            same, tile, (((1,), (1,)), ((), ())), preferred_element_type=jnp.float32
        )
        out_ref[:, pair * TAPS : (pair + 1) * TAPS] = turned.astype(jnp.bfloat16)


def place(pieces):
    sections, count, half, length = pieces.shape
    step = 16
    return pl.pallas_call(
        place_kernel,
        grid=(count // step,),
        in_specs=[pl.BlockSpec((sections, step, half, length), lambda i: (0, i, 0, 0))],
        out_specs=pl.BlockSpec((length, step * sections * half), lambda i: (0, i)),
        out_shape=jax.ShapeDtypeStruct((length, count * sections * half), jnp.bfloat16),
        name="place",
    )(pieces)


def swap_bit(value, bit, count):
    return lax.ppermute(value, "section", [(i, i ^ bit) for i in range(count)])


def per_device(slab_rows, filter_taps, skip_weights):
    sections = lax.axis_size("section")
    seq = lax.axis_size("seq")
    section = lax.axis_index("section")
    sec = section.astype(jnp.int32).reshape(1)

    own_params = jnp.concatenate(
        [filter_taps[0], jnp.pad(skip_weights, ((0, 3), (0, TAPS - skip_weights.shape[1])))], axis=0
    )
    params = own_params[None]
    for bit in (1, 2, 4):
        params = jnp.concatenate([params, swap_bit(params, bit, sections)], axis=0)
    params = params.reshape(sections * 8, TAPS)

    picked = pick(sec, slab_rows)
    moved = lax.all_to_all(
        picked.reshape(seq, HALF, TAPS), "seq", split_axis=0, concat_axis=0, tiled=True
    )
    outputs, info = chain(sec, moved.reshape(seq * HALF, TAPS), params, sections)
    pieces = lax.all_to_all(
        outputs.reshape(sections * seq, HALF, TAPS),
        ("section", "seq"),
        split_axis=0,
        concat_axis=0,
        tiled=True,
    )

    info = info.reshape(2, 2, 2, INFO, TAPS)
    for axis, bit in ((2, 1), (1, 2), (0, 4)):
        keep, send = jnp.split(info, 2, axis=axis)
        info = jnp.concatenate([keep, swap_bit(send, bit, sections)], axis=axis)
    for axis, bit in ((2, 1), (1, 2), (0, 4)):
        info = jnp.where((section & bit) != 0, jnp.flip(info, axis), info)
    info = info.reshape(sections // 2, 2, INFO, TAPS)
    groups_here = sections // 2
    before = info[:, :, :HALF, ::-1].reshape(groups_here, GROUP, TAPS)
    last = info[:, :, HALF:EDGE, ::-1].reshape(groups_here, GROUP, TAPS)
    lags = jnp.sum(info[:, :, EDGE : EDGE + 3].astype(jnp.float32), axis=(1, 2))
    running = jnp.einsum(
        "gci,gcl->gil", last, jnp.concatenate([last, before], axis=2),
        preferred_element_type=jnp.float32,
    )
    is_last = (jnp.arange(TAPS) == TAPS - 1)[None, :, None]
    running = running + jnp.where(is_last, jnp.pad(lags, ((0, 0), (TAPS - 1, 1)))[:, None], 0.0)
    offset = 1
    while offset < TAPS:
        running = running + jnp.pad(
            running[:, offset:, offset:], ((0, 0), (0, offset), (0, offset))
        )
        offset = offset * 2
    upper = running[:, :, :TAPS]
    ahead = jnp.arange(TAPS)[None, :] >= jnp.arange(TAPS)[:, None]
    hessians = jnp.where(ahead[None], upper, jnp.swapaxes(upper, 1, 2))
    hessians = hessians * (2.0 / (seq * TAPS * GROUP))

    restored = place(pieces.reshape(sections, seq, HALF, TAPS))
    return (restored[None], hessians[None])


def solution(mesh):
    in_specs = (P("seq", None), P("section", "seq", None), P("section", "seq"))
    out_specs = (P("section", "seq", None), P("section", "seq", None, None))
    return jax.shard_map(
        per_device, mesh=mesh, in_specs=in_specs, out_specs=out_specs, check_vma=False
    )
```

time: 338 us -> 132 us (0.39); the launches traced: 334 us -> 132 us
  local copies, waits for them, and re-layouts: 136 us -> 3.96 us
  matrix products: 24.9 us -> 0.27 us
  other arithmetic: 22.6 us -> 1.94 us
  starting transfers between devices: 82 us -> 61.4 us
  waiting for transfers between devices: 66.6 us -> 47 us
  Pallas kernels: 0 us -> 16.3 us
    gather x2 -> x0, local copies, waits for them, and re-layouts: 121 us -> none  [toeplitz(): tap_table = taps_row[:, jnp.clip(lag_index, 0, TAPS - 1)]]
    ppermute x11 -> x6, starting transfers between devices: 47.9 us -> 20.9 us  [swap_bit(): return lax.ppermute(value, 'section', [(i, i ^ bit) for i in range(count)])]
    dot_general x55 -> x1, matrix products: 24.9 us -> 0.27 us  [per_device(): jnp.einsum('gci,gcl->gil', last, jnp.concatenate([last, before], axis=2),...]
    pallas_call x0 -> x3, Pallas kernels: none -> 16.3 us  [the longest x1 8.87 us: chain(): pl.pallas_call(chain_kernel, grid_spec=pltpu.PrefetchScalarGridSpec(num_s...]
    all_to_all x2, waiting for transfers between devices: 47.3 us -> 34.9 us  [the longest x1 34.9 us: per_device(): lax.all_to_all(outputs.reshape(sections * seq, HALF, TAPS), ('section', '...]
    select_n x12 -> x3, other arithmetic: 11.9 us -> 0.06 us  [per_device(): info = jnp.where(section & bit != 0, jnp.flip(info, axis), info)]
    ppermute x11 -> x6, waiting for transfers between devices: 19.3 us -> 12.1 us  [swap_bit(): return lax.ppermute(value, 'section', [(i, i ^ bit) for i in range(count)])]
    all_to_all x2, starting transfers between devices: 34.1 us -> 40.5 us  [the longest x1 21.4 us: per_device(): lax.all_to_all(outputs.reshape(sections * seq, HALF, TAPS), ('section', '...]
  transfers between devices with their start and end apart: 13 -> 8, of which waited for: 12 -> 7; matrix products, arithmetic and copies ran while one was open for 43% -> 3% of each run, Pallas kernels for 0% -> 0%
where the time goes in v1:
time: 132 us
  starting transfers between devices  61.4 us (47%)
  waiting for transfers between devices  47 us (36%)
  Pallas kernels  16.3 us (12%)
  local copies, waits for them, and re-layouts  3.96 us (3%)
  other arithmetic  1.94 us (1%)
    all_to_all x1, waiting for transfers between devices, per_device(): lax.all_to_all(outputs.reshape(sections * seq, HALF, TAPS), ('section', '...  34.9 us
    all_to_all x1, starting transfers between devices, per_device(): lax.all_to_all(outputs.reshape(sections * seq, HALF, TAPS), ('section', '...  21.4 us
    ppermute x6, starting transfers between devices, swap_bit(): return lax.ppermute(value, 'section', [(i, i ^ bit) for i in range(count)])  20.9 us
    all_to_all x1, starting transfers between devices, per_device(): lax.all_to_all(picked.reshape(seq, HALF, TAPS), 'seq', split_axis=0, conc...  19.1 us
    ppermute x6, waiting for transfers between devices, swap_bit(): return lax.ppermute(value, 'section', [(i, i ^ bit) for i in range(count)])  12.1 us
    pallas_call x1, Pallas kernels, chain(): pl.pallas_call(chain_kernel, grid_spec=pltpu.PrefetchScalarGridSpec(num_s...  8.87 us
    pallas_call x1, Pallas kernels, place(): pl.pallas_call(place_kernel, grid=(count // step,), in_specs=[pl.BlockSpe...  3.93 us
    pallas_call x1, Pallas kernels, pick(): pl.pallas_call(pick_kernel, grid_spec=pltpu.PrefetchScalarGridSpec(num_sc...  3.55 us
  transfers between devices with their start and end apart: 8, of which 7 were waited for; matrix products, arithmetic and copies ran while one was open for 3% of the time, Pallas kernels for 0%

profile of v1, /device:TPU:1, one launch (start us, length us, event | category | flops | bytes accessed | tf_op | source)
XLA Modules:
  0.0 131.9 jit_solution(4631364978632883619)
XLA Ops:
  0.6 3.5 %pick.1 = bf16[512,128]{1,0:T(8,128)(2,1)} custom-call(s32[1]{0:T(128)} %bitcast.sec_ref, bf16[128,4096]{1,0:T(8,128)(2,1)} %slab_ref.1), custom_call_target="tpu_custom_call" | custom-call | tf_op jit(solution)/shard_map/pick/pallas_call | solution.py:41
  4.2 19.1 %all-to-all-start = ((bf16[64,8,128]{2,1,0:T(8,128)(2,1)}), bf16[64,8,128]{2,1,0:T(8,128)(2,1)S(1)}, u32[]{:S(2)}, u32[]{:S(2)}) async-start(bf16[64,8,128]{2,1,0:T(8,128)(2,1)} %bitcast.27), calls=%async_computation | async-start | bytes 262144 | tf_op jit(solution)/shard_map/all_to_all | solution.py:181
  23.3 0.7 copy-done.3
  24.0 2.9 %collective-permute-start = (bf16[1,8,128]{2,1,0:T(8,128)(2,1)S(1)}, bf16[1,8,128]{2,1,0:T(8,128)(2,1)S(1)}, u32[]{:S(2)}, u32[]{:S(2)}) collective-permute-start(bf16[1,8,128]{2,1,0:T(8,128)(2,1)S(1)} %fusion.9), channel_id=1, source_target_pairs={{0,64},{64,0},{128,192},{192,128},{256,320},{320,256},{384,448},{4... | collective-permute-start | bytes 6152 | tf_op jit(solution)/shard_map/ppermute | solution.py:163
  26.9 0.8 collective-permute-done
  27.7 3.2 %collective-permute-start.1 = (bf16[2,8,128]{2,1,0:T(8,128)(2,1)S(1)}, bf16[2,8,128]{2,1,0:T(8,128)(2,1)S(1)}, u32[]{:S(2)}, u32[]{:S(2)}) collective-permute-start(bf16[2,8,128]{2,1,0:T(8,128)(2,1)S(1)} %pad_maximum_fusion.4), channel_id=1, source_target_pairs={{0,128},{64,192},{128,0},{192,64},{256,384},{320,448},{384,256},{4... | collective-permute-start | bytes 12296 | tf_op jit(solution)/shard_map/ppermute | solution.py:163
  30.9 1.4 %collective-permute-done.1 = bf16[2,8,128]{2,1,0:T(8,128)(2,1)S(1)} collective-permute-done((bf16[2,8,128]{2,1,0:T(8,128)(2,1)S(1)}, bf16[2,8,128]{2,1,0:T(8,128)(2,1)S(1)}, u32[]{:S(2)}, u32[]{:S(2)}) %collective-permute-start.1) | collective-permute-done | bytes 4128 | tf_op jit(solution)/shard_map/ppermute | solution.py:163
  32.3 4.8 %collective-permute-start.2 = (bf16[4,8,128]{2,1,0:T(8,128)(2,1)S(1)}, bf16[4,8,128]{2,1,0:T(8,128)(2,1)S(1)}, u32[]{:S(2)}, u32[]{:S(2)}) collective-permute-start(bf16[4,8,128]{2,1,0:T(8,128)(2,1)S(1)} %pad_maximum_fusion.3), channel_id=1, source_target_pairs={{0,256},{64,320},{128,384},{192,448},{256,0},{320,64},{384,128},{4... | collective-permute-start | bytes 24584 | tf_op jit(solution)/shard_map/ppermute | solution.py:163
  37.1 1.4 %collective-permute-done.2 = bf16[4,8,128]{2,1,0:T(8,128)(2,1)S(1)} collective-permute-done((bf16[4,8,128]{2,1,0:T(8,128)(2,1)S(1)}, bf16[4,8,128]{2,1,0:T(8,128)(2,1)S(1)}, u32[]{:S(2)}, u32[]{:S(2)}) %collective-permute-start.2) | collective-permute-done | bytes 8224 | tf_op jit(solution)/shard_map/ppermute | solution.py:163
  38.5 0.6 maximum_bitcast_fusion.par_ref
  39.1 0.7 copy-done.1
  39.8 8.9 %chain.1 = (bf16[8,512,128]{2,1,0:T(8,128)(2,1)}, bf16[8,32,128]{2,1,0:T(8,128)(2,1)}) custom-call(s32[1]{0:T(128)} %bitcast.sec_ref, bf16[512,128]{1,0:T(8,128)(2,1)} %bitcast.28, bf16[64,128]{1,0:T(8,128)(2,1)} %maximum_bitcast_fusion.par_ref), custom_call_target="tpu_custom_call" | custom-call | tf_op jit(solution)/shard_map/chain/pallas_call | solution.py:112
  48.6 21.4 %all-to-all-start.1 = ((bf16[512,8,128]{2,1,0:T(8,128)(2,1)}), bf16[512,8,128]{2,1,0:T(8,128)(2,1)S(1)}, u32[]{:S(2)}, u32[]{:S(2)}) async-start(bf16[512,8,128]{2,1,0:T(8,128)(2,1)} %bitcast.25), calls=%async_computation.1 | async-start | bytes 2097152 | tf_op jit(solution)/shard_map/all_to_all | solution.py:185
  70.1 6.2 %collective-permute-start.3 = (bf16[2,2,1,32,128]{4,3,2,1,0:T(8,128)(2,1)S(1)}, bf16[2,2,1,32,128]{4,3,2,1,0:T(8,128)(2,1)S(1)}, u32[]{:S(2)}, u32[]{:S(2)}) collective-permute-start(bf16[2,2,1,32,128]{4,3,2,1,0:T(8,128)(2,1)S(1)} %get-tuple-element.13), channel_id=1, source_target_pairs={{0,64},{64,0},{128,192},{192,128},{256,320},{320,256},{384,448},{4... | collective-permute-start | bytes 98312 | tf_op jit(solution)/shard_map/ppermute | solution.py:163
  76.3 0.8 collective-permute-done.3
  77.2 1.9 %collective-permute-start.4 = (bf16[2,1,2,32,128]{4,3,2,1,0:T(8,128)(2,1)S(1)}, bf16[2,1,2,32,128]{4,3,2,1,0:T(8,128)(2,1)S(1)}, u32[]{:S(2)}, u32[]{:S(2)}) collective-permute-start(bf16[2,1,2,32,128]{4,3,2,1,0:T(8,128)(2,1)S(1)} %get-tuple-element.11), channel_id=1, source_target_pairs={{0,128},{64,192},{128,0},{192,64},{256,384},{320,448},{384,256},{4... | collective-permute-start | bytes 98312 | tf_op jit(solution)/shard_map/ppermute | solution.py:163
  79.1 3.1 %collective-permute-done.4 = bf16[2,1,2,32,128]{4,3,2,1,0:T(8,128)(2,1)S(1)} collective-permute-done((bf16[2,1,2,32,128]{4,3,2,1,0:T(8,128)(2,1)S(1)}, bf16[2,1,2,32,128]{4,3,2,1,0:T(8,128)(2,1)S(1)}, u32[]{:S(2)}, u32[]{:S(2)}) %collective-permute-start.4) | collective-permute-done | bytes 32800 | tf_op jit(solution)/shard_map/ppermute | solution.py:163
  82.2 1.9 %collective-permute-start.5 = (bf16[1,2,2,32,128]{4,3,2,1,0:T(8,128)(2,1)S(1)}, bf16[1,2,2,32,128]{4,3,2,1,0:T(8,128)(2,1)S(1)}, u32[]{:S(2)}, u32[]{:S(2)}) collective-permute-start(bf16[1,2,2,32,128]{4,3,2,1,0:T(8,128)(2,1)S(1)} %get-tuple-element.9), channel_id=1, source_target_pairs={{0,256},{64,320},{128,384},{192,448},{256,0},{320,64},{384,128},{4... | collective-permute-start | bytes 98312 | tf_op jit(solution)/shard_map/ppermute | solution.py:163
  84.1 4.6 %collective-permute-done.5 = bf16[1,2,2,32,128]{4,3,2,1,0:T(8,128)(2,1)S(1)} collective-permute-done((bf16[1,2,2,32,128]{4,3,2,1,0:T(8,128)(2,1)S(1)}, bf16[1,2,2,32,128]{4,3,2,1,0:T(8,128)(2,1)S(1)}, u32[]{:S(2)}, u32[]{:S(2)}) %collective-permute-start.5) | collective-permute-done | bytes 32800 | tf_op jit(solution)/shard_map/ppermute | solution.py:163
  89.1 0.3 convolution_add_fusion
  89.4 0.2 slice.47
  89.7 0.2 slice.48
  90.0 0.2 slice.49
  90.3 0.2 slice.50
  90.5 0.2 slice.51
  90.8 0.2 slice.52
  91.0 0.1 slice.53
  91.2 0.1 copy.5
  91.3 0.7 fusion.1
  92.1 34.9 %all-to-all-done.1 = bf16[512,8,128]{2,1,0:T(8,128)(2,1)S(1)} async-done(((bf16[512,8,128]{2,1,0:T(8,128)(2,1)}), bf16[512,8,128]{2,1,0:T(8,128)(2,1)S(1)}, u32[]{:S(2)}, u32[]{:S(2)}) %all-to-all-start.1) | async-done | bytes 1048608 | tf_op jit(solution)/shard_map/all_to_all | solution.py:185
  127.0 1.0 copy-done
  127.9 3.9 %place.1 = bf16[128,4096]{1,0:T(8,128)(2,1)} custom-call(bf16[8,64,8,128]{3,2,1,0:T(8,128)(2,1)} %bitcast.24), custom_call_target="tpu_custom_call" | custom-call | tf_op jit(solution)/shard_map/place/pallas_call | solution.py:152
  (32 shorter events, 0.9 us)
Async XLA Ops:
  4.2 34.9 %all-to-all-start = ((bf16[64,8,128]{2,1,0:T(8,128)(2,1)}), bf16[64,8,128]{2,1,0:T(8,128)(2,1)S(1)}, u32[]{:S(2)}, u32[]{:S(2)}) async-start(bf16[64,8,128]{2,1,0:T(8,128)(2,1)} %bitcast.27), calls=%async_computation | async-start | bytes 262144 | tf_op jit(solution)/shard_map/all_to_all | solution.py:181
  23.3 0.7 copy-start.3
  23.3 0.7 copy-start.4
  24.0 3.7 %collective-permute-start = (bf16[1,8,128]{2,1,0:T(8,128)(2,1)S(1)}, bf16[1,8,128]{2,1,0:T(8,128)(2,1)S(1)}, u32[]{:S(2)}, u32[]{:S(2)}) collective-permute-start(bf16[1,8,128]{2,1,0:T(8,128)(2,1)S(1)} %fusion.9), channel_id=1, source_target_pairs={{0,64},{64,0},{128,192},{192,128},{256,320},{320,256},{384,448},{4... | collective-permute-start | bytes 6152 | tf_op jit(solution)/shard_map/ppermute | solution.py:163
  27.7 4.6 %collective-permute-start.1 = (bf16[2,8,128]{2,1,0:T(8,128)(2,1)S(1)}, bf16[2,8,128]{2,1,0:T(8,128)(2,1)S(1)}, u32[]{:S(2)}, u32[]{:S(2)}) collective-permute-start(bf16[2,8,128]{2,1,0:T(8,128)(2,1)S(1)} %pad_maximum_fusion.4), channel_id=1, source_target_pairs={{0,128},{64,192},{128,0},{192,64},{256,384},{320,448},{384,256},{4... | collective-permute-start | bytes 12296 | tf_op jit(solution)/shard_map/ppermute | solution.py:163
  32.3 6.2 %collective-permute-start.2 = (bf16[4,8,128]{2,1,0:T(8,128)(2,1)S(1)}, bf16[4,8,128]{2,1,0:T(8,128)(2,1)S(1)}, u32[]{:S(2)}, u32[]{:S(2)}) collective-permute-start(bf16[4,8,128]{2,1,0:T(8,128)(2,1)S(1)} %pad_maximum_fusion.3), channel_id=1, source_target_pairs={{0,256},{64,320},{128,384},{192,448},{256,0},{320,64},{384,128},{4... | collective-permute-start | bytes 24584 | tf_op jit(solution)/shard_map/ppermute | solution.py:163
  39.1 0.7 copy-start.1
  48.6 21.4 %copy-start.2 = (bf16[8,32,128]{2,1,0:T(8,128)(2,1)S(1)}, bf16[8,32,128]{2,1,0:T(8,128)(2,1)}, u32[]{:S(2)}) copy-start(bf16[8,32,128]{2,1,0:T(8,128)(2,1)} %get-tuple-element.5) | copy-start | bytes 196612
  48.6 78.3 %all-to-all-start.1 = ((bf16[512,8,128]{2,1,0:T(8,128)(2,1)}), bf16[512,8,128]{2,1,0:T(8,128)(2,1)S(1)}, u32[]{:S(2)}, u32[]{:S(2)}) async-start(bf16[512,8,128]{2,1,0:T(8,128)(2,1)} %bitcast.25), calls=%async_computation.1 | async-start | bytes 2097152 | tf_op jit(solution)/shard_map/all_to_all | solution.py:185
  70.1 7.1 %collective-permute-start.3 = (bf16[2,2,1,32,128]{4,3,2,1,0:T(8,128)(2,1)S(1)}, bf16[2,2,1,32,128]{4,3,2,1,0:T(8,128)(2,1)S(1)}, u32[]{:S(2)}, u32[]{:S(2)}) collective-permute-start(bf16[2,2,1,32,128]{4,3,2,1,0:T(8,128)(2,1)S(1)} %get-tuple-element.13), channel_id=1, source_target_pairs={{0,64},{64,0},{128,192},{192,128},{256,320},{320,256},{384,448},{4... | collective-permute-start | bytes 98312 | tf_op jit(solution)/shard_map/ppermute | solution.py:163
  77.2 5.0 %collective-permute-start.4 = (bf16[2,1,2,32,128]{4,3,2,1,0:T(8,128)(2,1)S(1)}, bf16[2,1,2,32,128]{4,3,2,1,0:T(8,128)(2,1)S(1)}, u32[]{:S(2)}, u32[]{:S(2)}) collective-permute-start(bf16[2,1,2,32,128]{4,3,2,1,0:T(8,128)(2,1)S(1)} %get-tuple-element.11), channel_id=1, source_target_pairs={{0,128},{64,192},{128,0},{192,64},{256,384},{320,448},{384,256},{4... | collective-permute-start | bytes 98312 | tf_op jit(solution)/shard_map/ppermute | solution.py:163
  82.2 6.5 %collective-permute-start.5 = (bf16[1,2,2,32,128]{4,3,2,1,0:T(8,128)(2,1)S(1)}, bf16[1,2,2,32,128]{4,3,2,1,0:T(8,128)(2,1)S(1)}, u32[]{:S(2)}, u32[]{:S(2)}) collective-permute-start(bf16[1,2,2,32,128]{4,3,2,1,0:T(8,128)(2,1)S(1)} %get-tuple-element.9), channel_id=1, source_target_pairs={{0,256},{64,320},{128,384},{192,448},{256,0},{320,64},{384,128},{4... | collective-permute-start | bytes 98312 | tf_op jit(solution)/shard_map/ppermute | solution.py:163
  127.0 1.0 copy-start

commit v2 on v1

v2 whole, which is shorter than its diff:
```python
import jax
import jax.numpy as jnp
from jax import lax
from jax.experimental import pallas as pl
from jax.experimental.pallas import tpu as pltpu
from jax.sharding import PartitionSpec as P

GROUP = 16
TAPS = 128
HALF = 8
EDGE = 2 * HALF
INFO = 2 * EDGE
PARTS = 4
CHUNK = 1024
VMEM_LIMIT = 16 * 1024 * 1024


def limits():
    return pltpu.CompilerParams(vmem_limit_bytes=VMEM_LIMIT)


def pick_kernel(sec_ref, slab_ref, out_ref):
    sec = sec_ref[0]
    width = 256
    rows = width // 8
    out_row = lax.broadcasted_iota(jnp.int32, (rows, width), 0)
    lane = lax.broadcasted_iota(jnp.int32, (rows, width), 1)
    wanted = (out_row // HALF) * 64 + sec * HALF + out_row % HALF
    chosen = jnp.where(lane == wanted, 1.0, 0.0).astype(jnp.bfloat16)
    for piece in range(slab_ref.shape[1] // width):
        turned = lax.dot_general(
            chosen,
            slab_ref[:, piece * width : (piece + 1) * width],
            (((1,), (1,)), ((), ())),
            preferred_element_type=jnp.float32,
        )
        out_ref[piece * rows : (piece + 1) * rows, :] = turned.astype(jnp.bfloat16)


def pick(sec, slab_rows):
    length, width = slab_rows.shape
    return pl.pallas_call(
        pick_kernel,
        in_specs=[pl.BlockSpec(memory_space=pltpu.SMEM), pl.BlockSpec(memory_space=pltpu.VMEM)],
        out_specs=pl.BlockSpec(memory_space=pltpu.VMEM),
        out_shape=jax.ShapeDtypeStruct((width // 8, length), jnp.bfloat16),
        compiler_params=limits(),
        name="pick",
    )(sec, slab_rows)


def chain_kernel(sec_ref, x_ref, par_ref, out_ref, par, y_ref, sems):
    sec = sec_ref[0]
    sections, rows, _ = y_ref.shape
    par[...] = par_ref[...].astype(jnp.float32)
    lane = lax.broadcasted_iota(jnp.int32, (HALF, TAPS), 1)
    chan = lax.broadcasted_iota(jnp.int32, (HALF, TAPS), 0)
    blank = jnp.zeros((HALF, TAPS), jnp.float32)
    current_b = x_ref[...]
    copies = []
    for step in range(sections):
        slot = sec ^ step
        taps_row = par[pl.ds(slot * 8 + sec // 2, 1), :]
        skip_row = par[pl.ds(slot * 8 + 4, 1), :]
        spread = jnp.concatenate([taps_row, jnp.zeros_like(taps_row)], axis=1)
        spread = jnp.broadcast_to(spread, (TAPS, 2 * TAPS))
        band = pltpu.roll(spread, 0, 1, stride=1, stride_axis=0).astype(jnp.bfloat16)
        own = jnp.where(lane == sec * HALF + chan, jnp.broadcast_to(skip_row, (HALF, TAPS)), 0.0)
        gain = jnp.broadcast_to(jnp.sum(own, axis=1, keepdims=True), (HALF, TAPS))
        both = jnp.dot(current_b, band, preferred_element_type=jnp.float32)
        carried = jnp.concatenate([blank, both[: rows - HALF, TAPS:]], axis=0)
        current = current_b.astype(jnp.float32)
        direct = (current.reshape(rows // HALF, HALF, TAPS) * gain[None]).reshape(rows, TAPS)
        current_b = (both[:, :TAPS] + carried + direct).astype(jnp.bfloat16)
        y_ref[step] = current_b
        copies.append(pltpu.make_async_copy(y_ref.at[step], out_ref.at[step], sems.at[step]))
        copies[-1].start()
    for copy in copies:
        copy.wait()


def chain(sec, rows_in, params, sections):
    rows = rows_in.shape[0]
    return pl.pallas_call(
        chain_kernel,
        in_specs=[pl.BlockSpec(memory_space=pltpu.SMEM)] + [pl.BlockSpec(memory_space=pltpu.VMEM)] * 2,
        out_specs=pl.BlockSpec(memory_space=pl.ANY),
        out_shape=jax.ShapeDtypeStruct((sections, rows, TAPS), jnp.bfloat16),
        scratch_shapes=[
            pltpu.VMEM(params.shape, jnp.float32),
            pltpu.VMEM((sections, rows, TAPS), jnp.bfloat16),
            pltpu.SemaphoreType.DMA((sections,)),
        ],
        compiler_params=limits(),
        name="chain",
    )(sec, rows_in, params)


def lags_kernel(sec_ref, x_ref, y_ref, info_ref):
    sec = sec_ref[0]
    sections, rows, _ = y_ref.shape
    blank = jnp.zeros((HALF, TAPS), jnp.float32)

    def one(step, source):
        current_b = source
        current = current_b.astype(jnp.float32)
        body = jnp.concatenate([current[: rows - HALF], blank], axis=0)
        after = jnp.concatenate([body[HALF:], blank], axis=0)
        pair = jnp.concatenate([body, after], axis=1).astype(jnp.bfloat16)
        gram = lax.dot_general(
            current_b, pair, (((0,), (0,)), ((), ())), preferred_element_type=jnp.float32
        )
        size = TAPS
        while size > 8:
            size = size // 2
            gram = gram[:size] + pltpu.roll(gram[size:], 2 * TAPS - size, 1)
        row = lax.broadcasted_iota(jnp.int32, gram.shape, 0)
        for bit in (4, 2, 1):
            gram = jnp.where((row & bit) != 0, pltpu.roll(gram, 2 * TAPS - bit, 1), gram)
        lags = jnp.sum(gram, axis=0, keepdims=True)[:, :TAPS]
        high = lags.astype(jnp.bfloat16).astype(jnp.float32)
        middle = (lags - high).astype(jnp.bfloat16).astype(jnp.float32)
        low = lags - high - middle
        info_row = lax.broadcasted_iota(jnp.int32, (INFO - EDGE, TAPS), 0)
        packed = jnp.where(
            info_row == 0,
            high,
            jnp.where(info_row == 1, middle, jnp.where(info_row == 2, low, 0.0)),
        )
        info = jnp.concatenate([current[rows - EDGE :], packed], axis=0)
        info_ref[step ^ sec] = info.astype(jnp.bfloat16)

    one(0, x_ref[...])

    @pl.loop(1, sections)
    def _(step):
        one(step, y_ref[step - 1])


def lag_info(sec, rows_in, outputs):
    sections, rows, _ = outputs.shape
    return pl.pallas_call(
        lags_kernel,
        in_specs=[pl.BlockSpec(memory_space=pltpu.SMEM)] + [pl.BlockSpec(memory_space=pltpu.VMEM)] * 2,
        out_specs=pl.BlockSpec(memory_space=pltpu.VMEM),
        out_shape=jax.ShapeDtypeStruct((sections, INFO, TAPS), jnp.bfloat16),
        compiler_params=limits(),
        cost_estimate=pl.CostEstimate(
            flops=sections * 4 * rows * TAPS * TAPS, bytes_accessed=2 * outputs.size, transcendentals=0
        ),
        name="lags",
    )(sec, rows_in, outputs)


def place_kernel(x_ref, out_ref, turned, sems):
    quads = x_ref.shape[1]
    share = quads // PARTS
    copies = []
    for part in range(PARTS):
        for pair in range(part * share // 2, (part + 1) * share // 2):
            parts = [x_ref[r, 2 * pair + half] for half in range(2) for r in range(8)]
            tile = jnp.concatenate(parts, axis=0)
            turned[:, pair * TAPS : (pair + 1) * TAPS] = tile.T
        span = pl.ds(part * CHUNK, CHUNK)
        copies.append(pltpu.make_async_copy(turned.at[:, span], out_ref.at[:, span], sems.at[part]))
        copies[-1].start()
    for copy in copies:
        copy.wait()


def place(pieces):
    sections, count, half, length = pieces.shape
    width = count * sections * half
    return pl.pallas_call(
        place_kernel,
        in_specs=[pl.BlockSpec(memory_space=pltpu.VMEM)],
        out_specs=pl.BlockSpec(memory_space=pl.ANY),
        out_shape=jax.ShapeDtypeStruct((length, width), jnp.bfloat16),
        scratch_shapes=[pltpu.VMEM((length, width), jnp.bfloat16), pltpu.SemaphoreType.DMA((PARTS,))],
        compiler_params=limits(),
        name="place",
    )(pieces)


def swap_bit(value, bit, count):
    return lax.ppermute(value, "section", [(i, i ^ bit) for i in range(count)])


def per_device(slab_rows, filter_taps, skip_weights):
    sections = lax.axis_size("section")
    seq = lax.axis_size("seq")
    section = lax.axis_index("section")
    sec = section.astype(jnp.int32).reshape(1)

    own_params = jnp.concatenate(
        [filter_taps[0], jnp.pad(skip_weights, ((0, 3), (0, TAPS - skip_weights.shape[1])))], axis=0
    )
    params = own_params[None]
    params = jnp.concatenate([params, swap_bit(params, 1, sections)], axis=0)
    params = jnp.concatenate([params] + [swap_bit(params, bits, sections) for bits in (2, 4, 6)], axis=0)
    params = params.reshape(sections * 8, TAPS)

    picked = pick(sec, slab_rows)
    moved = lax.all_to_all(
        picked.reshape(seq, HALF, TAPS), "seq", split_axis=0, concat_axis=0, tiled=True
    )
    rows_in = moved.reshape(seq * HALF, TAPS)
    outputs = chain(sec, rows_in, params, sections)
    pieces = lax.all_to_all(
        outputs.reshape(sections * seq, HALF, TAPS),
        ("section", "seq"),
        split_axis=0,
        concat_axis=0,
        tiled=True,
    )

    info = lag_info(sec, rows_in, outputs).reshape(2, 2, 2, INFO, TAPS)
    for axis, bit in ((2, 1), (1, 2), (0, 4)):
        keep, send = jnp.split(info, 2, axis=axis)
        info = jnp.concatenate([keep, swap_bit(send, bit, sections)], axis=axis)
    for axis, bit in ((2, 1), (1, 2), (0, 4)):
        info = jnp.where((section & bit) != 0, jnp.flip(info, axis), info)
    info = info.reshape(sections // 2, 2, INFO, TAPS)
    groups_here = sections // 2
    before = info[:, :, :HALF, ::-1].reshape(groups_here, GROUP, TAPS)
    last = info[:, :, HALF:EDGE, ::-1].reshape(groups_here, GROUP, TAPS)
    lags = jnp.sum(info[:, :, EDGE : EDGE + 3].astype(jnp.float32), axis=(1, 2))
    running = jnp.einsum(
        "gci,gcl->gil", last, jnp.concatenate([last, before], axis=2),
        preferred_element_type=jnp.float32,
    )
    is_last = (jnp.arange(TAPS) == TAPS - 1)[None, :, None]
    running = running + jnp.where(is_last, jnp.pad(lags, ((0, 0), (TAPS - 1, 1)))[:, None], 0.0)
    offset = 1
    while offset < TAPS:
        running = running + jnp.pad(
            running[:, offset:, offset:], ((0, 0), (0, offset), (0, offset))
        )
        offset = offset * 2
    upper = running[:, :, :TAPS]
    ahead = jnp.arange(TAPS)[None, :] >= jnp.arange(TAPS)[:, None]
    hessians = jnp.where(ahead[None], upper, jnp.swapaxes(upper, 1, 2))
    hessians = hessians * (2.0 / (seq * TAPS * GROUP))

    restored = place(pieces.reshape(sections, seq, HALF, TAPS))
    return (restored[None], hessians[None])


def solution(mesh):
    in_specs = (P("seq", None), P("section", "seq", None), P("section", "seq"))
    out_specs = (P("section", "seq", None), P("section", "seq", None, None))
    return jax.shard_map(
        per_device, mesh=mesh, in_specs=in_specs, out_specs=out_specs, check_vma=False
    )
```

time: 132 us -> 118 us (0.89)
  Pallas kernels: 16.3 us -> 11.2 us
  waiting for transfers between devices: 47 us -> 42.1 us
  starting transfers between devices: 61.4 us -> 58.3 us
    all_to_all x1, waiting for transfers between devices: 34.9 us -> 27.7 us  [per_device(): lax.all_to_all(outputs.reshape(sections * seq, HALF, TAPS), ('section', '...]
    ppermute x6 -> x7, starting transfers between devices: 20.9 us -> 27.8 us  [swap_bit(): return lax.ppermute(value, 'section', [(i, i ^ bit) for i in range(count)])]
    all_to_all x1, starting transfers between devices: 19.1 us -> 12.9 us  [per_device(): lax.all_to_all(picked.reshape(seq, HALF, TAPS), 'seq', split_axis=0, conc...]
    pallas_call x3 -> x4, Pallas kernels: 16.3 us -> 11.2 us  [the longest x1 7.06 us: lag_info(): pl.pallas_call(lags_kernel, in_specs=[pl.BlockSpec(memory_space=pltpu.SME...]
    all_to_all x1, starting transfers between devices: 21.4 us -> 17.5 us  [per_device(): lax.all_to_all(outputs.reshape(sections * seq, HALF, TAPS), ('section', '...]
    all_to_all x1, waiting for transfers between devices: 0.01 us -> 3.27 us  [per_device(): lax.all_to_all(picked.reshape(seq, HALF, TAPS), 'seq', split_axis=0, conc...]
    ppermute x6 -> x7, waiting for transfers between devices: 12.1 us -> 11.2 us  [swap_bit(): return lax.ppermute(value, 'section', [(i, i ^ bit) for i in range(count)])]
  transfers between devices with their start and end apart: 8 -> 9, of which waited for: 7 -> 6; matrix products, arithmetic and copies ran while one was open for 3% -> 3% of each run, Pallas kernels for 0% -> 7%
where the time goes in v2:
time: 118 us
  starting transfers between devices  58.3 us (49%)
  waiting for transfers between devices  42.1 us (36%)
  Pallas kernels  11.2 us (9%)
  local copies, waits for them, and re-layouts  3.58 us (3%)
  other arithmetic  1.33 us (1%)
    ppermute x7, starting transfers between devices, swap_bit(): return lax.ppermute(value, 'section', [(i, i ^ bit) for i in range(count)])  27.8 us
    all_to_all x1, waiting for transfers between devices, per_device(): lax.all_to_all(outputs.reshape(sections * seq, HALF, TAPS), ('section', '...  27.7 us
    all_to_all x1, starting transfers between devices, per_device(): lax.all_to_all(outputs.reshape(sections * seq, HALF, TAPS), ('section', '...  17.5 us
    all_to_all x1, starting transfers between devices, per_device(): lax.all_to_all(picked.reshape(seq, HALF, TAPS), 'seq', split_axis=0, conc...  12.9 us
    ppermute x7, waiting for transfers between devices, swap_bit(): return lax.ppermute(value, 'section', [(i, i ^ bit) for i in range(count)])  11.2 us
    pallas_call x1, Pallas kernels, lag_info(): pl.pallas_call(lags_kernel, in_specs=[pl.BlockSpec(memory_space=pltpu.SME...  7.06 us
    all_to_all x1, waiting for transfers between devices, per_device(): lax.all_to_all(picked.reshape(seq, HALF, TAPS), 'seq', split_axis=0, conc...  3.27 us
  transfers between devices with their start and end apart: 9, of which 6 were waited for; matrix products, arithmetic and copies ran while one was open for 3% of the time, Pallas kernels for 7%

profile of v2, /device:TPU:1, one launch (start us, length us, event | category | flops | bytes accessed | tf_op | source)
XLA Modules:
  0.0 117.8 jit_solution(12456532537968962996)
XLA Ops:
  0.6 0.6 copy-done.2
  1.3 8.7 %collective-permute-start = (bf16[1,8,128]{2,1,0:T(8,128)(2,1)S(1)}, bf16[1,8,128]{2,1,0:T(8,128)(2,1)S(1)}, u32[]{:S(2)}, u32[]{:S(2)}) collective-permute-start(bf16[1,8,128]{2,1,0:T(8,128)(2,1)S(1)} %fusion.9), channel_id=1, source_target_pairs={{0,64},{64,0},{128,192},{192,128},{256,320},{320,256},{384,448},{4... | collective-permute-start | bytes 6152 | tf_op jit(solution)/shard_map/ppermute | solution.py:186
  10.1 1.2 %copy-done = bf16[128,4096]{1,0:T(8,128)(2,1)S(1)} copy-done((bf16[128,4096]{1,0:T(8,128)(2,1)S(1)}, bf16[128,4096]{1,0:T(8,128)(2,1)}, u32[]{:S(2)}) %copy-start) | copy-done | bytes 1048600
  11.3 1.1 pick.1
  12.4 12.9 %all-to-all-start = ((bf16[64,8,128]{2,1,0:T(8,128)(2,1)}), bf16[64,8,128]{2,1,0:T(8,128)(2,1)S(1)}, u32[]{:S(2)}, u32[]{:S(2)}) async-start(bf16[64,8,128]{2,1,0:T(8,128)(2,1)} %bitcast.1), calls=%async_computation | async-start | bytes 262144 | tf_op jit(solution)/shard_map/all_to_all | solution.py:204
  25.4 4.6 %collective-permute-start.3 = (bf16[2,8,128]{2,1,0:T(8,128)(2,1)S(1)}, bf16[2,8,128]{2,1,0:T(8,128)(2,1)S(1)}, u32[]{:S(2)}, u32[]{:S(2)}) collective-permute-start(bf16[2,8,128]{2,1,0:T(8,128)(2,1)S(1)} %pad_maximum_fusion.3), channel_id=1, source_target_pairs={{0,384},{64,448},{128,256},{192,320},{256,128},{320,192},{384,0},{... | collective-permute-start | bytes 12296 | tf_op jit(solution)/shard_map/ppermute | solution.py:186
  30.1 2.3 %collective-permute-start.2 = (bf16[2,8,128]{2,1,0:T(8,128)(2,1)S(1)}, bf16[2,8,128]{2,1,0:T(8,128)(2,1)S(1)}, u32[]{:S(2)}, u32[]{:S(2)}) collective-permute-start(bf16[2,8,128]{2,1,0:T(8,128)(2,1)S(1)} %pad_maximum_fusion.3), channel_id=1, source_target_pairs={{0,256},{64,320},{128,384},{192,448},{256,0},{320,64},{384,128},{4... | collective-permute-start | bytes 12296 | tf_op jit(solution)/shard_map/ppermute | solution.py:186
  32.3 2.1 %collective-permute-start.1 = (bf16[2,8,128]{2,1,0:T(8,128)(2,1)S(1)}, bf16[2,8,128]{2,1,0:T(8,128)(2,1)S(1)}, u32[]{:S(2)}, u32[]{:S(2)}) collective-permute-start(bf16[2,8,128]{2,1,0:T(8,128)(2,1)S(1)} %pad_maximum_fusion.3), channel_id=1, source_target_pairs={{0,128},{64,192},{128,0},{192,64},{256,384},{320,448},{384,256},{4... | collective-permute-start | bytes 12296 | tf_op jit(solution)/shard_map/ppermute | solution.py:186
  34.5 2.5 %collective-permute-done.1 = bf16[2,8,128]{2,1,0:T(8,128)(2,1)S(1)} collective-permute-done((bf16[2,8,128]{2,1,0:T(8,128)(2,1)S(1)}, bf16[2,8,128]{2,1,0:T(8,128)(2,1)S(1)}, u32[]{:S(2)}, u32[]{:S(2)}) %collective-permute-start.1) | collective-permute-done | bytes 4128 | tf_op jit(solution)/shard_map/ppermute | solution.py:186
  37.0 3.3 %all-to-all-done = bf16[64,8,128]{2,1,0:T(8,128)(2,1)S(1)} async-done(((bf16[64,8,128]{2,1,0:T(8,128)(2,1)}), bf16[64,8,128]{2,1,0:T(8,128)(2,1)S(1)}, u32[]{:S(2)}, u32[]{:S(2)}) %all-to-all-start) | async-done | bytes 131104 | tf_op jit(solution)/shard_map/all_to_all | solution.py:204
  40.3 1.9 %chain.1.y_ref = bf16[8,512,128]{2,1,0:T(8,128)(2,1)} custom-call(s32[1]{0:T(128)} %bitcast.sec_ref, bf16[512,128]{1,0:T(8,128)(2,1)S(1)} %bitcast.26, bf16[64,128]{1,0:T(8,128)(2,1)S(1)} %bitcast.29), custom_call_target="tpu_custom_call" | custom-call | tf_op jit(solution)/shard_map/chain/pallas_call | solution.py:84
  42.2 17.5 %all-to-all-start.1 = ((bf16[512,8,128]{2,1,0:T(8,128)(2,1)}), bf16[512,8,128]{2,1,0:T(8,128)(2,1)S(1)}, u32[]{:S(2)}, u32[]{:S(2)}) async-start(bf16[512,8,128]{2,1,0:T(8,128)(2,1)} %bitcast.6), calls=%async_computation.1 | async-start | bytes 2097152 | tf_op jit(solution)/shard_map/all_to_all | solution.py:209
  59.8 7.1 %lags.1 = bf16[8,32,128]{2,1,0:T(8,128)(2,1)S(1)} custom-call(s32[1]{0:T(128)} %bitcast.sec_ref, bf16[512,128]{1,0:T(8,128)(2,1)S(1)} %bitcast.27, bf16[8,512,128]{2,1,0:T(8,128)(2,1)} %chain.1.y_ref), custom_call_target="tpu_custom_call" | custom-call | flops 268435456 | bytes 1048576 | tf_op jit(solution)/shard_map/lags/pallas_call | solution.py:142
  66.8 6.2 %collective-permute-start.4 = (bf16[2,2,1,32,128]{4,3,2,1,0:T(8,128)(2,1)S(1)}, bf16[2,2,1,32,128]{4,3,2,1,0:T(8,128)(2,1)S(1)}, u32[]{:S(2)}, u32[]{:S(2)}) collective-permute-start(bf16[2,2,1,32,128]{4,3,2,1,0:T(8,128)(2,1)S(1)} %get-tuple-element.9), channel_id=1, source_target_pairs={{0,64},{64,0},{128,192},{192,128},{256,320},{320,256},{384,448},{4... | collective-permute-start | bytes 98312 | tf_op jit(solution)/shard_map/ppermute | solution.py:186
  73.1 0.8 collective-permute-done.4
  73.9 1.9 %collective-permute-start.5 = (bf16[2,1,2,32,128]{4,3,2,1,0:T(8,128)(2,1)S(1)}, bf16[2,1,2,32,128]{4,3,2,1,0:T(8,128)(2,1)S(1)}, u32[]{:S(2)}, u32[]{:S(2)}) collective-permute-start(bf16[2,1,2,32,128]{4,3,2,1,0:T(8,128)(2,1)S(1)} %get-tuple-element.7), channel_id=1, source_target_pairs={{0,128},{64,192},{128,0},{192,64},{256,384},{320,448},{384,256},{4... | collective-permute-start | bytes 98312 | tf_op jit(solution)/shard_map/ppermute | solution.py:186
  75.8 3.2 %collective-permute-done.5 = bf16[2,1,2,32,128]{4,3,2,1,0:T(8,128)(2,1)S(1)} collective-permute-done((bf16[2,1,2,32,128]{4,3,2,1,0:T(8,128)(2,1)S(1)}, bf16[2,1,2,32,128]{4,3,2,1,0:T(8,128)(2,1)S(1)}, u32[]{:S(2)}, u32[]{:S(2)}) %collective-permute-start.5) | collective-permute-done | bytes 32800 | tf_op jit(solution)/shard_map/ppermute | solution.py:186
  79.0 1.9 %collective-permute-start.6 = (bf16[1,2,2,32,128]{4,3,2,1,0:T(8,128)(2,1)S(1)}, bf16[1,2,2,32,128]{4,3,2,1,0:T(8,128)(2,1)S(1)}, u32[]{:S(2)}, u32[]{:S(2)}) collective-permute-start(bf16[1,2,2,32,128]{4,3,2,1,0:T(8,128)(2,1)S(1)} %get-tuple-element.5), channel_id=1, source_target_pairs={{0,256},{64,320},{128,384},{192,448},{256,0},{320,64},{384,128},{4... | collective-permute-start | bytes 98312 | tf_op jit(solution)/shard_map/ppermute | solution.py:186
  81.0 4.7 %collective-permute-done.6 = bf16[1,2,2,32,128]{4,3,2,1,0:T(8,128)(2,1)S(1)} collective-permute-done((bf16[1,2,2,32,128]{4,3,2,1,0:T(8,128)(2,1)S(1)}, bf16[1,2,2,32,128]{4,3,2,1,0:T(8,128)(2,1)S(1)}, u32[]{:S(2)}, u32[]{:S(2)}) %collective-permute-start.6) | collective-permute-done | bytes 32800 | tf_op jit(solution)/shard_map/ppermute | solution.py:186
  85.8 0.1 rev.22
  86.0 0.3 convolution_add_fusion
  86.3 0.2 slice.47
  86.6 0.2 slice.48
  86.9 0.2 slice.49
  87.2 0.2 slice.50
  87.4 0.2 slice.51
  87.7 0.2 slice.52
  87.9 0.1 slice.53
  88.1 0.1 copy.5
  88.2 0.7 fusion.1
  89.0 27.7 %all-to-all-done.1 = bf16[512,8,128]{2,1,0:T(8,128)(2,1)S(1)} async-done(((bf16[512,8,128]{2,1,0:T(8,128)(2,1)}), bf16[512,8,128]{2,1,0:T(8,128)(2,1)S(1)}, u32[]{:S(2)}, u32[]{:S(2)}) %all-to-all-start.1) | async-done | bytes 1048608 | tf_op jit(solution)/shard_map/all_to_all | solution.py:209
  116.7 1.1 place.1
  (34 shorter events, 0.9 us)
Async XLA Ops:
  0.6 0.7 copy-start.2
  0.6 0.7 copy-start.1
  1.3 24.1 %collective-permute-start = (bf16[1,8,128]{2,1,0:T(8,128)(2,1)S(1)}, bf16[1,8,128]{2,1,0:T(8,128)(2,1)S(1)}, u32[]{:S(2)}, u32[]{:S(2)}) collective-permute-start(bf16[1,8,128]{2,1,0:T(8,128)(2,1)S(1)} %fusion.9), channel_id=1, source_target_pairs={{0,64},{64,0},{128,192},{192,128},{256,320},{320,256},{384,448},{4... | collective-permute-start | bytes 6152 | tf_op jit(solution)/shard_map/ppermute | solution.py:186
  10.1 1.2 %copy-start = (bf16[128,4096]{1,0:T(8,128)(2,1)S(1)}, bf16[128,4096]{1,0:T(8,128)(2,1)}, u32[]{:S(2)}) copy-start(bf16[128,4096]{1,0:T(8,128)(2,1)} %slab_ref.1) | copy-start | bytes 3145732
  12.4 27.9 %all-to-all-start = ((bf16[64,8,128]{2,1,0:T(8,128)(2,1)}), bf16[64,8,128]{2,1,0:T(8,128)(2,1)S(1)}, u32[]{:S(2)}, u32[]{:S(2)}) async-start(bf16[64,8,128]{2,1,0:T(8,128)(2,1)} %bitcast.1), calls=%async_computation | async-start | bytes 262144 | tf_op jit(solution)/shard_map/all_to_all | solution.py:204
  25.4 11.6 %collective-permute-start.3 = (bf16[2,8,128]{2,1,0:T(8,128)(2,1)S(1)}, bf16[2,8,128]{2,1,0:T(8,128)(2,1)S(1)}, u32[]{:S(2)}, u32[]{:S(2)}) collective-permute-start(bf16[2,8,128]{2,1,0:T(8,128)(2,1)S(1)} %pad_maximum_fusion.3), channel_id=1, source_target_pairs={{0,384},{64,448},{128,256},{192,320},{256,128},{320,192},{384,0},{... | collective-permute-start | bytes 12296 | tf_op jit(solution)/shard_map/ppermute | solution.py:186
  30.1 6.9 %collective-permute-start.2 = (bf16[2,8,128]{2,1,0:T(8,128)(2,1)S(1)}, bf16[2,8,128]{2,1,0:T(8,128)(2,1)S(1)}, u32[]{:S(2)}, u32[]{:S(2)}) collective-permute-start(bf16[2,8,128]{2,1,0:T(8,128)(2,1)S(1)} %pad_maximum_fusion.3), channel_id=1, source_target_pairs={{0,256},{64,320},{128,384},{192,448},{256,0},{320,64},{384,128},{4... | collective-permute-start | bytes 12296 | tf_op jit(solution)/shard_map/ppermute | solution.py:186
  32.3 4.6 %collective-permute-start.1 = (bf16[2,8,128]{2,1,0:T(8,128)(2,1)S(1)}, bf16[2,8,128]{2,1,0:T(8,128)(2,1)S(1)}, u32[]{:S(2)}, u32[]{:S(2)}) collective-permute-start(bf16[2,8,128]{2,1,0:T(8,128)(2,1)S(1)} %pad_maximum_fusion.3), channel_id=1, source_target_pairs={{0,128},{64,192},{128,0},{192,64},{256,384},{320,448},{384,256},{4... | collective-permute-start | bytes 12296 | tf_op jit(solution)/shard_map/ppermute | solution.py:186
  42.2 74.4 %all-to-all-start.1 = ((bf16[512,8,128]{2,1,0:T(8,128)(2,1)}), bf16[512,8,128]{2,1,0:T(8,128)(2,1)S(1)}, u32[]{:S(2)}, u32[]{:S(2)}) async-start(bf16[512,8,128]{2,1,0:T(8,128)(2,1)} %bitcast.6), calls=%async_computation.1 | async-start | bytes 2097152 | tf_op jit(solution)/shard_map/all_to_all | solution.py:209
  66.8 7.1 %collective-permute-start.4 = (bf16[2,2,1,32,128]{4,3,2,1,0:T(8,128)(2,1)S(1)}, bf16[2,2,1,32,128]{4,3,2,1,0:T(8,128)(2,1)S(1)}, u32[]{:S(2)}, u32[]{:S(2)}) collective-permute-start(bf16[2,2,1,32,128]{4,3,2,1,0:T(8,128)(2,1)S(1)} %get-tuple-element.9), channel_id=1, source_target_pairs={{0,64},{64,0},{128,192},{192,128},{256,320},{320,256},{384,448},{4... | collective-permute-start | bytes 98312 | tf_op jit(solution)/shard_map/ppermute | solution.py:186
  73.9 5.1 %collective-permute-start.5 = (bf16[2,1,2,32,128]{4,3,2,1,0:T(8,128)(2,1)S(1)}, bf16[2,1,2,32,128]{4,3,2,1,0:T(8,128)(2,1)S(1)}, u32[]{:S(2)}, u32[]{:S(2)}) collective-permute-start(bf16[2,1,2,32,128]{4,3,2,1,0:T(8,128)(2,1)S(1)} %get-tuple-element.7), channel_id=1, source_target_pairs={{0,128},{64,192},{128,0},{192,64},{256,384},{320,448},{384,256},{4... | collective-permute-start | bytes 98312 | tf_op jit(solution)/shard_map/ppermute | solution.py:186
  79.0 6.6 %collective-permute-start.6 = (bf16[1,2,2,32,128]{4,3,2,1,0:T(8,128)(2,1)S(1)}, bf16[1,2,2,32,128]{4,3,2,1,0:T(8,128)(2,1)S(1)}, u32[]{:S(2)}, u32[]{:S(2)}) collective-permute-start(bf16[1,2,2,32,128]{4,3,2,1,0:T(8,128)(2,1)S(1)} %get-tuple-element.5), channel_id=1, source_target_pairs={{0,256},{64,320},{128,384},{192,448},{256,0},{320,64},{384,128},{4... | collective-permute-start | bytes 98312 | tf_op jit(solution)/shard_map/ppermute | solution.py:186

commit v3 on v2

v3 whole, which is shorter than its diff:
```python
import jax
import jax.numpy as jnp
from jax import lax
from jax.experimental import pallas as pl
from jax.experimental.pallas import tpu as pltpu
from jax.sharding import Mesh, PartitionSpec as P

GROUP = 16
TAPS = 128
QUARTERS = 4
WIDE = 32
SPAN = 256
EDGE = 2 * GROUP
INFO = EDGE + 16
MIB = 1024 * 1024
EVERY = ("section", "x", "quarter", "slot")


def limits(mib):
    return pltpu.CompilerParams(vmem_limit_bytes=mib * MIB)


def pick_kernel(sec_ref, slab_ref, out_ref, held, sems):
    sec = sec_ref[0]
    copies = []
    for x in range(4):
        start = pl.multiple_of(x * 1024 + (sec // 2) * SPAN, SPAN)
        copies.append(pltpu.make_async_copy(slab_ref.at[:, pl.ds(start, SPAN)], held.at[x], sems.at[x]))
        copies[-1].start()
    rows = SPAN // 2
    out_row = lax.broadcasted_iota(jnp.int32, (rows, SPAN), 0)
    lane = lax.broadcasted_iota(jnp.int32, (rows, SPAN), 1)
    wanted = (out_row // WIDE) * 64 + (sec % 2) * WIDE + out_row % WIDE
    chosen = jnp.where(lane == wanted, 1.0, 0.0).astype(jnp.bfloat16)
    for x in range(4):
        copies[x].wait()
        turned = lax.dot_general(
            chosen, held[x], (((1,), (1,)), ((), ())), preferred_element_type=jnp.float32
        ).astype(jnp.bfloat16)
        for quarter in range(QUARTERS):
            out_ref[x * QUARTERS + quarter] = turned


def pick(sec, slab_rows):
    length = slab_rows.shape[0]
    return pl.pallas_call(
        pick_kernel,
        in_specs=[pl.BlockSpec(memory_space=pltpu.SMEM), pl.BlockSpec(memory_space=pl.ANY)],
        out_specs=pl.BlockSpec(memory_space=pltpu.VMEM),
        out_shape=jax.ShapeDtypeStruct((4 * QUARTERS, SPAN // 2, length), jnp.bfloat16),
        scratch_shapes=[pltpu.VMEM((4, length, SPAN), jnp.bfloat16), pltpu.SemaphoreType.DMA((4,))],
        name="pick",
    )(sec, slab_rows)


def chain_kernel(where_ref, x_ref, par_ref, out_ref, kept_ref, par, y_ref, sems, kept_sems):
    sec = where_ref[0]
    quarter = where_ref[1]
    sections = out_ref.shape[0]
    blocks = x_ref.shape[0]
    share = 16
    par[...] = par_ref[...].astype(jnp.float32)
    lane = lax.broadcasted_iota(jnp.int32, (GROUP, TAPS), 1)
    chan = lax.broadcasted_iota(jnp.int32, (GROUP, TAPS), 0)
    copies = []
    for step in range(sections):
        slot = (step // 2) ^ quarter
        slot = 2 * slot + ((step % 2) ^ (sec % 2))

        def source(first, last, low):
            if step == 0:
                return x_ref[first:last, low : low + GROUP, :]
            return y_ref[step - 1, first:last, low : low + GROUP, :]

        skip_row = jnp.broadcast_to(par[pl.ds(slot * 8 + 4, 1), :], (GROUP, TAPS))
        for part in range(WIDE // GROUP):
            low = part * GROUP
            taps_row = par[pl.ds(slot * 8 + 2 * (sec % 2) + part, 1), :]
            spread = jnp.concatenate([taps_row, jnp.zeros_like(taps_row)], axis=1)
            spread = jnp.broadcast_to(spread, (TAPS, 2 * TAPS))
            band = pltpu.roll(spread, 0, 1, stride=1, stride_axis=0).astype(jnp.bfloat16)
            own = jnp.where(lane == (sec % 2) * WIDE + low + chan, skip_row, 0.0)
            gain = jnp.broadcast_to(jnp.sum(own, axis=1, keepdims=True), (GROUP, TAPS))
            carry = jnp.zeros((GROUP, TAPS), jnp.float32)
            for first in range(0, blocks, share):
                current = source(first, first + share, low).reshape(share * GROUP, TAPS)
                both = jnp.dot(current, band, preferred_element_type=jnp.float32)
                carried = jnp.concatenate([carry, both[: (share - 1) * GROUP, TAPS:]], axis=0)
                carry = both[(share - 1) * GROUP :, TAPS:]
                direct = current.astype(jnp.float32).reshape(share, GROUP, TAPS) * gain[None]
                filtered = both[:, :TAPS] + carried + direct.reshape(share * GROUP, TAPS)
                y_ref[step, first : first + share, low : low + GROUP, :] = filtered.astype(
                    jnp.bfloat16
                ).reshape(share, GROUP, TAPS)
        for x in range(4):
            begin = 16 * x + 4 * quarter
            copies.append(
                pltpu.make_async_copy(
                    y_ref.at[step, pl.ds(begin, 4)], out_ref.at[step, x], sems.at[step, x]
                )
            )
            copies[-1].start()
        if step + 1 < sections:
            copies.append(
                pltpu.make_async_copy(y_ref.at[step], kept_ref.at[step], kept_sems.at[step])
            )
            copies[-1].start()
    for copy in copies:
        copy.wait()


def chain(where, rows_in, params, sections):
    blocks = rows_in.shape[0]
    return pl.pallas_call(
        chain_kernel,
        in_specs=[pl.BlockSpec(memory_space=pltpu.SMEM)] + [pl.BlockSpec(memory_space=pltpu.VMEM)] * 2,
        out_specs=[pl.BlockSpec(memory_space=pl.ANY)] * 2,
        out_shape=[
            jax.ShapeDtypeStruct((sections, 4, 4, WIDE, TAPS), jnp.bfloat16),
            pltpu.HBM((sections - 1, blocks, WIDE, TAPS), jnp.bfloat16),
        ],
        scratch_shapes=[
            pltpu.VMEM(params.shape, jnp.float32),
            pltpu.VMEM((sections, blocks, WIDE, TAPS), jnp.bfloat16),
            pltpu.SemaphoreType.DMA((sections, 4)),
            pltpu.SemaphoreType.DMA((sections - 1,)),
        ],
        compiler_params=limits(24),
        name="chain",
    )(where, rows_in, params)


def lags_kernel(where_ref, x_ref, y_ref, info_ref):
    quarter = where_ref[1]
    sections, blocks = y_ref.shape[0] + 1, y_ref.shape[1]
    rows = (blocks - 1) * GROUP
    blank = jnp.zeros((GROUP, TAPS), jnp.bfloat16)
    for step in range(sections):
        slot = (step // 2) ^ quarter
        for part in range(WIDE // GROUP):
            low = part * GROUP
            if step == 0:
                whole = x_ref[:, low : low + GROUP, :]
            else:
                whole = y_ref[step - 1, :, low : low + GROUP, :]
            body = whole[: blocks - 1].reshape(rows, TAPS)
            after = jnp.concatenate([body[GROUP:], blank], axis=0)
            pair = jnp.concatenate([body, after], axis=1)
            gram = lax.dot_general(
                body, pair, (((0,), (0,)), ((), ())), preferred_element_type=jnp.float32
            )
            size = TAPS
            while size > 8:
                size = size // 2
                gram = gram[:size] + pltpu.roll(gram[size:], 2 * TAPS - size, 1)
            row = lax.broadcasted_iota(jnp.int32, gram.shape, 0)
            for bit in (4, 2, 1):
                gram = jnp.where((row & bit) != 0, pltpu.roll(gram, 2 * TAPS - bit, 1), gram)
            lags = jnp.sum(gram, axis=0, keepdims=True)[:, :TAPS]
            high = lags.astype(jnp.bfloat16).astype(jnp.float32)
            middle = (lags - high).astype(jnp.bfloat16).astype(jnp.float32)
            rest = lags - high - middle
            info_row = lax.broadcasted_iota(jnp.int32, (INFO - EDGE, TAPS), 0)
            packed = jnp.where(
                info_row == 0,
                high,
                jnp.where(info_row == 1, middle, jnp.where(info_row == 2, rest, 0.0)),
            )
            edge = whole[blocks - 2 :].reshape(EDGE, TAPS)
            piece = jnp.concatenate([edge, packed.astype(jnp.bfloat16)], axis=0)
            info_ref[slot, step % 2, part] = piece


def lag_info(where, rows_in, states):
    sections = states.shape[0] + 1
    return pl.pallas_call(
        lags_kernel,
        in_specs=[pl.BlockSpec(memory_space=pltpu.SMEM)] + [pl.BlockSpec(memory_space=pltpu.VMEM)] * 2,
        out_specs=pl.BlockSpec(memory_space=pltpu.VMEM),
        out_shape=jax.ShapeDtypeStruct((sections // 2, 2, WIDE // GROUP, INFO, TAPS), jnp.bfloat16),
        compiler_params=limits(16),
        cost_estimate=pl.CostEstimate(
            flops=4 * states.size * TAPS, bytes_accessed=2 * states.size, transcendentals=0
        ),
        name="lags",
    )(where, rows_in, states)


def place_kernel(x_ref, out_ref, turned, sems):
    copies = []
    for x in range(4):
        for fourth in range(4):
            for pair in range(2):
                parts = [
                    x_ref[2 * fourth + half, x, 2 * pair + slot]
                    for slot in range(2)
                    for half in range(2)
                ]
                tile = jnp.concatenate(parts, axis=0)
                at = 1024 * x + SPAN * fourth + TAPS * pair
                turned[:, at : at + TAPS] = tile.T
        span = pl.ds(x * 1024, 1024)
        copies.append(pltpu.make_async_copy(turned.at[:, span], out_ref.at[:, span], sems.at[x]))
        copies[-1].start()
    for copy in copies:
        copy.wait()


def place(pieces):
    width = pieces.size // TAPS
    return pl.pallas_call(
        place_kernel,
        in_specs=[pl.BlockSpec(memory_space=pltpu.VMEM)],
        out_specs=pl.BlockSpec(memory_space=pl.ANY),
        out_shape=jax.ShapeDtypeStruct((TAPS, width), jnp.bfloat16),
        scratch_shapes=[pltpu.VMEM((TAPS, width), jnp.bfloat16), pltpu.SemaphoreType.DMA((4,))],
        compiler_params=limits(16),
        name="place",
    )(pieces)


def device(section, x, quarter, slot):
    return ((section * 4 + x) * QUARTERS + quarter) * 4 + slot


def turn_params(value):
    pairs = []
    for x in range(4):
        for slot in range(4):
            for quarter in range(QUARTERS):
                for chip in range(4):
                    for core in range(2):
                        origin = device(2 * chip + core, x, quarter, slot)
                        pairs.append((origin, device(2 * quarter + core, x, chip, slot)))
    return lax.ppermute(value, EVERY, pairs)


def home_round(value, offset):
    pairs = []
    for x in range(4):
        for slot in range(4):
            for quarter in range(QUARTERS):
                for core in range(2):
                    origin = device(2 * quarter + core, x, quarter, slot)
                    pairs.append((origin, device(2 * (quarter ^ offset) + core, x, quarter, slot)))
    return lax.ppermute(value, EVERY, pairs)


def swap_cores(value):
    return lax.ppermute(value, "section", [(i, i ^ 1) for i in range(8)])


def per_device(slab_rows, filter_taps, skip_weights):
    sections = lax.axis_size("section")
    section = lax.axis_index("section").astype(jnp.int32)
    quarter = lax.axis_index("quarter").astype(jnp.int32)
    sec = section.reshape(1)
    where = jnp.stack([section, quarter])

    own_params = jnp.concatenate(
        [filter_taps[0], jnp.pad(skip_weights, ((0, 3), (0, TAPS - skip_weights.shape[1])))], axis=0
    )[None]
    params = jnp.concatenate([own_params, swap_cores(own_params)], axis=0)
    away = [
        lax.ppermute(params, "section", [(i, i ^ (2 * offset)) for i in range(8)])
        for offset in (1, 2, 3)
    ]
    params = jnp.concatenate([params] + away, axis=0)
    params = turn_params(params).reshape(sections * 8, TAPS)

    picked = pick(sec, slab_rows)
    moved = lax.all_to_all(
        picked.reshape(64, WIDE, TAPS), ("x", "quarter", "slot"), split_axis=0, concat_axis=0, tiled=True
    )
    outputs, states = chain(where, moved, params, sections)
    pieces = lax.all_to_all(
        outputs.reshape(sections * 16, WIDE, TAPS),
        ("section", "x", "slot"),
        split_axis=0,
        concat_axis=0,
        tiled=True,
    )

    info = lag_info(where, moved, states)
    local = jnp.where(section // 2 == quarter, info[0], jnp.zeros_like(info[0]))
    info = local + home_round(info[1], 1) + home_round(info[2], 2) + home_round(info[3], 3)
    odd = (section & 1) != 0
    mine = jnp.where(odd, info[1], info[0])
    partner = swap_cores(jnp.where(odd, info[0], info[1]))
    info = jnp.where(odd, jnp.concatenate([partner, mine]), jnp.concatenate([mine, partner]))
    before = info[:, :GROUP, ::-1]
    last = info[:, GROUP:EDGE, ::-1]
    lags = jnp.sum(info[:, EDGE : EDGE + 3].astype(jnp.float32), axis=1)
    running = jnp.einsum(
        "gci,gcl->gil", last, jnp.concatenate([last, before], axis=2),
        preferred_element_type=jnp.float32,
    )
    is_last = (jnp.arange(TAPS) == TAPS - 1)[None, :, None]
    running = running + jnp.where(is_last, jnp.pad(lags, ((0, 0), (TAPS - 1, 1)))[:, None], 0.0)
    offset = 1
    while offset < TAPS:
        running = running + jnp.pad(
            running[:, offset:, offset:], ((0, 0), (0, offset), (0, offset))
        )
        offset = offset * 2
    upper = running[:, :, :TAPS]
    ahead = jnp.arange(TAPS)[None, :] >= jnp.arange(TAPS)[:, None]
    hessians = jnp.where(ahead[None], upper, jnp.swapaxes(upper, 1, 2))
    hessians = hessians * (2.0 / (64 * TAPS * GROUP))

    restored = place(pieces.reshape(sections, 4, 4, WIDE, TAPS))
    return (restored[None], hessians[None])


def solution(mesh):
    split = Mesh(mesh.devices.reshape(8, 4, QUARTERS, 4), EVERY)
    seq = ("x", "quarter", "slot")
    in_specs = (P(seq, None), P("section", seq, None), P("section", seq))
    out_specs = (P("section", seq, None), P("section", seq, None, None))
    return jax.shard_map(
        per_device, mesh=split, in_specs=in_specs, out_specs=out_specs, check_vma=False
    )
```

time: 118 us -> 101 us (0.86)
  waiting for transfers between devices: 42.1 us -> 22.8 us
  Pallas kernels: 11.2 us -> 13.2 us
  starting transfers between devices: 58.3 us -> 56.8 us
  other arithmetic: 1.33 us -> 2.75 us
    all_to_all x2, waiting for transfers between devices: 30.9 us -> 16.8 us  [the longest x1 10.8 us: per_device(): lax.all_to_all(picked.reshape(64, WIDE, TAPS), ('x', 'quarter', 'slot'),...]
    ppermute x7 -> x9, waiting for transfers between devices: 11.2 us -> 6.01 us  [the longest x3 3.88 us: per_device(): lax.ppermute(params, 'section', [(i, i ^ 2 * offset) for i in range(8)])]
    ppermute x7 -> x9, starting transfers between devices: 27.8 us -> 23.3 us  [the longest x3 9.64 us: per_device(): lax.ppermute(params, 'section', [(i, i ^ 2 * offset) for i in range(8)])]
    all_to_all x2, starting transfers between devices: 30.5 us -> 33.4 us  [the longest x1 19.1 us: per_device(): lax.all_to_all(picked.reshape(64, WIDE, TAPS), ('x', 'quarter', 'slot'),...]
    pallas_call x1, Pallas kernels: 1.92 us -> 3.95 us  [chain(): pl.pallas_call(chain_kernel, in_specs=[pl.BlockSpec(memory_space=pltpu.SM...]
    pallas_call x1, Pallas kernels: 7.06 us -> 5.74 us  [lag_info(): pl.pallas_call(lags_kernel, in_specs=[pl.BlockSpec(memory_space=pltpu.SME...]
    pallas_call x1, Pallas kernels: 1.12 us -> 2.41 us  [pick(): pl.pallas_call(pick_kernel, in_specs=[pl.BlockSpec(memory_space=pltpu.SME...]
  transfers between devices with their start and end apart: 9 -> 11, of which waited for: 6 -> 6; matrix products, arithmetic and copies ran while one was open for 3% -> 5% of each run, Pallas kernels for 7% -> 6%
where the time goes in v3:
time: 101 us
  starting transfers between devices  56.8 us (56%)
  waiting for transfers between devices  22.8 us (23%)
  Pallas kernels  13.2 us (13%)
  local copies, waits for them, and re-layouts  3.72 us (4%)
  other arithmetic  2.75 us (3%)
    all_to_all x1, starting transfers between devices, per_device(): lax.all_to_all(picked.reshape(64, WIDE, TAPS), ('x', 'quarter', 'slot'),...  19.1 us
    all_to_all x1, starting transfers between devices, per_device(): lax.all_to_all(outputs.reshape(sections * 16, WIDE, TAPS), ('section', 'x...  14.3 us
    all_to_all x1, waiting for transfers between devices, per_device(): lax.all_to_all(picked.reshape(64, WIDE, TAPS), ('x', 'quarter', 'slot'),...  10.8 us
    ppermute x3, starting transfers between devices, per_device(): lax.ppermute(params, 'section', [(i, i ^ 2 * offset) for i in range(8)])  9.64 us
    ppermute x3, starting transfers between devices, home_round(): return lax.ppermute(value, EVERY, pairs)  7.14 us
    all_to_all x1, waiting for transfers between devices, per_device(): lax.all_to_all(outputs.reshape(sections * 16, WIDE, TAPS), ('section', 'x...  6.02 us
    ppermute x2, starting transfers between devices, swap_cores(): return lax.ppermute(value, 'section', [(i, i ^ 1) for i in range(8)])  5.9 us
    pallas_call x1, Pallas kernels, lag_info(): pl.pallas_call(lags_kernel, in_specs=[pl.BlockSpec(memory_space=pltpu.SME...  5.74 us
  transfers between devices with their start and end apart: 11, of which 6 were waited for; matrix products, arithmetic and copies ran while one was open for 5% of the time, Pallas kernels for 6%

profile of v3, /device:TPU:1, one launch (start us, length us, event | category | flops | bytes accessed | tf_op | source)
XLA Modules:
  0.0 100.6 jit_solution(4724020136605860340)
XLA Ops:
  0.6 2.4 %pick.1 = bf16[16,128,128]{2,1,0:T(8,128)(2,1)} custom-call(s32[1]{0:T(128)} %bitcast.sec_ref, bf16[128,4096]{1,0:T(8,128)(2,1)} %slab_ref.1), custom_call_target="tpu_custom_call" | custom-call | tf_op jit(solution)/shard_map/pick/pallas_call | solution.py:46
  3.0 19.1 %all-to-all-start = ((bf16[64,32,128]{2,1,0:T(8,128)(2,1)}), bf16[64,32,128]{2,1,0:T(8,128)(2,1)S(1)}, u32[]{:S(2)}, u32[]{:S(2)}) async-start(bf16[64,32,128]{2,1,0:T(8,128)(2,1)} %bitcast.41), calls=%async_computation | async-start | bytes 1048576 | tf_op jit(solution)/shard_map/all_to_all | solution.py:272
  22.2 0.7 fusion.11
  22.9 2.9 %collective-permute-start = (bf16[1,8,128]{2,1,0:T(8,128)(2,1)S(1)}, bf16[1,8,128]{2,1,0:T(8,128)(2,1)S(1)}, u32[]{:S(2)}, u32[]{:S(2)}) collective-permute-start(bf16[1,8,128]{2,1,0:T(8,128)(2,1)S(1)} %fusion.11), channel_id=1, source_target_pairs={{0,64},{64,0},{128,192},{192,128},{256,320},{320,256},{384,448},{4... | collective-permute-start | bytes 6152 | tf_op jit(solution)/shard_map/ppermute | solution.py:250
  25.7 0.7 constant_dynamic-update-slice_fusion.4
  26.5 3.2 %collective-permute-start.1 = (bf16[2,8,128]{2,1,0:T(8,128)(2,1)S(1)}, bf16[2,8,128]{2,1,0:T(8,128)(2,1)S(1)}, u32[]{:S(2)}, u32[]{:S(2)}) collective-permute-start(bf16[2,8,128]{2,1,0:T(8,128)(2,1)S(1)} %pad_maximum_fusion), channel_id=1, source_target_pairs={{0,128},{64,192},{128,0},{192,64},{256,384},{320,448},{384,256},{4... | collective-permute-start | bytes 12296 | tf_op jit(solution)/shard_map/ppermute | solution.py:265
  29.7 4.5 %collective-permute-start.2 = (bf16[2,8,128]{2,1,0:T(8,128)(2,1)S(1)}, bf16[2,8,128]{2,1,0:T(8,128)(2,1)S(1)}, u32[]{:S(2)}, u32[]{:S(2)}) collective-permute-start(bf16[2,8,128]{2,1,0:T(8,128)(2,1)S(1)} %pad_maximum_fusion), channel_id=1, source_target_pairs={{0,256},{64,320},{128,384},{192,448},{256,0},{320,64},{384,128},{4... | collective-permute-start | bytes 12296 | tf_op jit(solution)/shard_map/ppermute | solution.py:265
  34.3 1.9 %collective-permute-start.3 = (bf16[2,8,128]{2,1,0:T(8,128)(2,1)S(1)}, bf16[2,8,128]{2,1,0:T(8,128)(2,1)S(1)}, u32[]{:S(2)}, u32[]{:S(2)}) collective-permute-start(bf16[2,8,128]{2,1,0:T(8,128)(2,1)S(1)} %pad_maximum_fusion), channel_id=1, source_target_pairs={{0,384},{64,448},{128,256},{192,320},{256,128},{320,192},{384,0},{... | collective-permute-start | bytes 12296 | tf_op jit(solution)/shard_map/ppermute | solution.py:265
  36.3 3.9 %collective-permute-done.3 = bf16[2,8,128]{2,1,0:T(8,128)(2,1)S(1)} collective-permute-done((bf16[2,8,128]{2,1,0:T(8,128)(2,1)S(1)}, bf16[2,8,128]{2,1,0:T(8,128)(2,1)S(1)}, u32[]{:S(2)}, u32[]{:S(2)}) %collective-permute-start.3) | collective-permute-done | bytes 4128 | tf_op jit(solution)/shard_map/ppermute | solution.py:265
  40.1 0.7 collective-permute-start.4
  40.9 10.8 %all-to-all-done.x_ref = bf16[64,32,128]{2,1,0:T(8,128)(2,1)S(1)} async-done(((bf16[64,32,128]{2,1,0:T(8,128)(2,1)}), bf16[64,32,128]{2,1,0:T(8,128)(2,1)S(1)}, u32[]{:S(2)}, u32[]{:S(2)}) %all-to-all-start) | async-done | bytes 524320 | tf_op jit(solution)/shard_map/all_to_all | solution.py:272
  51.7 4.0 %chain.1 = (bf16[8,4,4,32,128]{4,3,2,1,0:T(8,128)(2,1)}, bf16[7,64,32,128]{3,2,1,0:T(8,128)(2,1)}) custom-call(s32[2]{0:T(128)S(1)} %pad_add_fusion.7.where_ref, bf16[64,32,128]{2,1,0:T(8,128)(2,1)S(1)} %all-to-all-done.x_ref, bf16[64,128]{1,0:T(8,128)(2,1)S(1)} %bitcast.40), custom_call_target="tpu_custom_call" | custom-call | tf_op jit(solution)/shard_map/chain/pallas_call | solution.py:114
  55.7 14.3 %all-to-all-start.1 = ((bf16[128,32,128]{2,1,0:T(8,128)(2,1)}), bf16[128,32,128]{2,1,0:T(8,128)(2,1)S(1)}, u32[]{:S(2)}, u32[]{:S(2)}) async-start(bf16[128,32,128]{2,1,0:T(8,128)(2,1)} %bitcast.6), calls=%async_computation.1 | async-start | bytes 2097152 | tf_op jit(solution)/shard_map/all_to_all | solution.py:276
  70.0 2.0 %copy-done = bf16[7,64,32,128]{3,2,1,0:T(8,128)(2,1)S(1)} copy-done((bf16[7,64,32,128]{3,2,1,0:T(8,128)(2,1)S(1)}, bf16[7,64,32,128]{3,2,1,0:T(8,128)(2,1)}, u32[]{:S(2)}) %copy-start) | copy-done | bytes 3670040
  72.0 5.7 %lags.1 = bf16[4,2,2,48,128]{4,3,2,1,0:T(8,128)(2,1)S(1)} custom-call(s32[2]{0:T(128)S(1)} %pad_add_fusion.7.where_ref, bf16[64,32,128]{2,1,0:T(8,128)(2,1)S(1)} %all-to-all-done.x_ref, bf16[7,64,32,128]{3,2,1,0:T(8,128)(2,1)S(1)} %copy-done), custom_call_target="tpu_custom_call" | custom-call | flops 939524096 | bytes 3670016 | tf_op jit(solution)/shard_map/lags/pallas_call | solution.py:176
  77.8 3.5 %collective-permute-start.5 = (bf16[2,2,48,128]{3,2,1,0:T(8,128)(2,1)S(1)}, bf16[2,2,48,128]{3,2,1,0:T(8,128)(2,1)S(1)}, u32[]{:S(2)}, u32[]{:S(2)}) collective-permute-start(bf16[2,2,48,128]{3,2,1,0:T(8,128)(2,1)S(1)} %get-tuple-element.6), channel_id=1, source_target_pairs={{0,128},{64,192},{132,4},{196,68},{264,392},{328,456},{396,268},{4... | collective-permute-start | bytes 147464 | tf_op jit(solution)/shard_map/ppermute | solution.py:246
  81.3 2.4 %collective-permute-start.6 = (bf16[2,2,48,128]{3,2,1,0:T(8,128)(2,1)S(1)}, bf16[2,2,48,128]{3,2,1,0:T(8,128)(2,1)S(1)}, u32[]{:S(2)}, u32[]{:S(2)}) collective-permute-start(bf16[2,2,48,128]{3,2,1,0:T(8,128)(2,1)S(1)} %get-tuple-element.8), channel_id=1, source_target_pairs={{0,256},{64,320},{132,388},{196,452},{264,8},{328,72},{396,140},{4... | collective-permute-start | bytes 147464 | tf_op jit(solution)/shard_map/ppermute | solution.py:246
  83.7 1.3 %collective-permute-start.7 = (bf16[2,2,48,128]{3,2,1,0:T(8,128)(2,1)S(1)}, bf16[2,2,48,128]{3,2,1,0:T(8,128)(2,1)S(1)}, u32[]{:S(2)}, u32[]{:S(2)}) collective-permute-start(bf16[2,2,48,128]{3,2,1,0:T(8,128)(2,1)S(1)} %get-tuple-element.7), channel_id=1, source_target_pairs={{0,384},{64,448},{132,260},{196,324},{264,136},{328,200},{396,12},... | collective-permute-start | bytes 147464 | tf_op jit(solution)/shard_map/ppermute | solution.py:246
  85.0 1.2 %collective-permute-done.7 = bf16[2,2,48,128]{3,2,1,0:T(8,128)(2,1)S(1)} collective-permute-done((bf16[2,2,48,128]{3,2,1,0:T(8,128)(2,1)S(1)}, bf16[2,2,48,128]{3,2,1,0:T(8,128)(2,1)S(1)}, u32[]{:S(2)}, u32[]{:S(2)}) %collective-permute-start.7) | collective-permute-done | bytes 49184 | tf_op jit(solution)/shard_map/ppermute | solution.py:246
  86.3 3.0 %collective-permute-start.8 = (bf16[2,48,128]{2,1,0:T(8,128)(2,1)S(1)}, bf16[2,48,128]{2,1,0:T(8,128)(2,1)S(1)}, u32[]{:S(2)}, u32[]{:S(2)}) collective-permute-start(bf16[2,48,128]{2,1,0:T(8,128)(2,1)S(1)} %get-tuple-element.11), channel_id=1, source_target_pairs={{0,64},{64,0},{128,192},{192,128},{256,320},{320,256},{384,448},{4... | collective-permute-start | bytes 73736 | tf_op jit(solution)/shard_map/ppermute | solution.py:250
  89.3 0.8 collective-permute-done.8
  90.5 0.3 convolution_add_fusion
  90.7 0.2 slice.79
  91.0 0.2 slice.80
  91.3 0.2 slice.81
  91.6 0.2 slice.82
  91.9 0.2 slice.83
  92.1 0.2 slice.84
  92.5 0.1 copy.5
  92.7 0.7 fusion.1
  93.4 6.0 %all-to-all-done.1 = bf16[128,32,128]{2,1,0:T(8,128)(2,1)S(1)} async-done(((bf16[128,32,128]{2,1,0:T(8,128)(2,1)}), bf16[128,32,128]{2,1,0:T(8,128)(2,1)S(1)}, u32[]{:S(2)}, u32[]{:S(2)}) %all-to-all-start.1) | async-done | bytes 1048608 | tf_op jit(solution)/shard_map/all_to_all | solution.py:276
  99.4 1.1 %place.1 = bf16[128,4096]{1,0:T(8,128)(2,1)} custom-call(bf16[8,4,4,32,128]{4,3,2,1,0:T(8,128)(2,1)S(1)} %bitcast.39), custom_call_target="tpu_custom_call" | custom-call | tf_op jit(solution)/shard_map/place/pallas_call | solution.py:211
  (32 shorter events, 1.1 us)
Async XLA Ops:
  3.0 48.6 %all-to-all-start = ((bf16[64,32,128]{2,1,0:T(8,128)(2,1)}), bf16[64,32,128]{2,1,0:T(8,128)(2,1)S(1)}, u32[]{:S(2)}, u32[]{:S(2)}) async-start(bf16[64,32,128]{2,1,0:T(8,128)(2,1)} %bitcast.41), calls=%async_computation | async-start | bytes 1048576 | tf_op jit(solution)/shard_map/all_to_all | solution.py:272
  22.9 3.7 %collective-permute-start = (bf16[1,8,128]{2,1,0:T(8,128)(2,1)S(1)}, bf16[1,8,128]{2,1,0:T(8,128)(2,1)S(1)}, u32[]{:S(2)}, u32[]{:S(2)}) collective-permute-start(bf16[1,8,128]{2,1,0:T(8,128)(2,1)S(1)} %fusion.11), channel_id=1, source_target_pairs={{0,64},{64,0},{128,192},{192,128},{256,320},{320,256},{384,448},{4... | collective-permute-start | bytes 6152 | tf_op jit(solution)/shard_map/ppermute | solution.py:250
  26.5 9.7 %collective-permute-start.1 = (bf16[2,8,128]{2,1,0:T(8,128)(2,1)S(1)}, bf16[2,8,128]{2,1,0:T(8,128)(2,1)S(1)}, u32[]{:S(2)}, u32[]{:S(2)}) collective-permute-start(bf16[2,8,128]{2,1,0:T(8,128)(2,1)S(1)} %pad_maximum_fusion), channel_id=1, source_target_pairs={{0,128},{64,192},{128,0},{192,64},{256,384},{320,448},{384,256},{4... | collective-permute-start | bytes 12296 | tf_op jit(solution)/shard_map/ppermute | solution.py:265
  29.7 6.5 %collective-permute-start.2 = (bf16[2,8,128]{2,1,0:T(8,128)(2,1)S(1)}, bf16[2,8,128]{2,1,0:T(8,128)(2,1)S(1)}, u32[]{:S(2)}, u32[]{:S(2)}) collective-permute-start(bf16[2,8,128]{2,1,0:T(8,128)(2,1)S(1)} %pad_maximum_fusion), channel_id=1, source_target_pairs={{0,256},{64,320},{128,384},{192,448},{256,0},{320,64},{384,128},{4... | collective-permute-start | bytes 12296 | tf_op jit(solution)/shard_map/ppermute | solution.py:265
  34.3 5.9 %collective-permute-start.3 = (bf16[2,8,128]{2,1,0:T(8,128)(2,1)S(1)}, bf16[2,8,128]{2,1,0:T(8,128)(2,1)S(1)}, u32[]{:S(2)}, u32[]{:S(2)}) collective-permute-start(bf16[2,8,128]{2,1,0:T(8,128)(2,1)S(1)} %pad_maximum_fusion), channel_id=1, source_target_pairs={{0,384},{64,448},{128,256},{192,320},{256,128},{320,192},{384,0},{... | collective-permute-start | bytes 12296 | tf_op jit(solution)/shard_map/ppermute | solution.py:265
  40.1 0.7 collective-permute-start.4
  55.7 43.8 %all-to-all-start.1 = ((bf16[128,32,128]{2,1,0:T(8,128)(2,1)}), bf16[128,32,128]{2,1,0:T(8,128)(2,1)S(1)}, u32[]{:S(2)}, u32[]{:S(2)}) async-start(bf16[128,32,128]{2,1,0:T(8,128)(2,1)} %bitcast.6), calls=%async_computation.1 | async-start | bytes 2097152 | tf_op jit(solution)/shard_map/all_to_all | solution.py:276
  70.0 2.0 %copy-start = (bf16[7,64,32,128]{3,2,1,0:T(8,128)(2,1)S(1)}, bf16[7,64,32,128]{3,2,1,0:T(8,128)(2,1)}, u32[]{:S(2)}) copy-start(bf16[7,64,32,128]{3,2,1,0:T(8,128)(2,1)} %get-tuple-element.5.y_ref) | copy-start | bytes 11010052
  77.8 7.2 %collective-permute-start.5 = (bf16[2,2,48,128]{3,2,1,0:T(8,128)(2,1)S(1)}, bf16[2,2,48,128]{3,2,1,0:T(8,128)(2,1)S(1)}, u32[]{:S(2)}, u32[]{:S(2)}) collective-permute-start(bf16[2,2,48,128]{3,2,1,0:T(8,128)(2,1)S(1)} %get-tuple-element.6), channel_id=1, source_target_pairs={{0,128},{64,192},{132,4},{196,68},{264,392},{328,456},{396,268},{4... | collective-permute-start | bytes 147464 | tf_op jit(solution)/shard_map/ppermute | solution.py:246
  81.3 3.7 %collective-permute-start.6 = (bf16[2,2,48,128]{3,2,1,0:T(8,128)(2,1)S(1)}, bf16[2,2,48,128]{3,2,1,0:T(8,128)(2,1)S(1)}, u32[]{:S(2)}, u32[]{:S(2)}) collective-permute-start(bf16[2,2,48,128]{3,2,1,0:T(8,128)(2,1)S(1)} %get-tuple-element.8), channel_id=1, source_target_pairs={{0,256},{64,320},{132,388},{196,452},{264,8},{328,72},{396,140},{4... | collective-permute-start | bytes 147464 | tf_op jit(solution)/shard_map/ppermute | solution.py:246
  83.7 2.6 %collective-permute-start.7 = (bf16[2,2,48,128]{3,2,1,0:T(8,128)(2,1)S(1)}, bf16[2,2,48,128]{3,2,1,0:T(8,128)(2,1)S(1)}, u32[]{:S(2)}, u32[]{:S(2)}) collective-permute-start(bf16[2,2,48,128]{3,2,1,0:T(8,128)(2,1)S(1)} %get-tuple-element.7), channel_id=1, source_target_pairs={{0,384},{64,448},{132,260},{196,324},{264,136},{328,200},{396,12},... | collective-permute-start | bytes 147464 | tf_op jit(solution)/shard_map/ppermute | solution.py:246
  86.3 3.9 %collective-permute-start.8 = (bf16[2,48,128]{2,1,0:T(8,128)(2,1)S(1)}, bf16[2,48,128]{2,1,0:T(8,128)(2,1)S(1)}, u32[]{:S(2)}, u32[]{:S(2)}) collective-permute-start(bf16[2,48,128]{2,1,0:T(8,128)(2,1)S(1)} %get-tuple-element.11), channel_id=1, source_target_pairs={{0,64},{64,0},{128,192},{192,128},{256,320},{320,256},{384,448},{4... | collective-permute-start | bytes 73736 | tf_op jit(solution)/shard_map/ppermute | solution.py:250

commit v4 on v3

--- a/solution.py
+++ b/solution.py
@@ -10,6 +10,8 @@
 QUARTERS = 4
 WIDE = 32
 SPAN = 256
+SERVED = 4
+HALO = 8
 EDGE = 2 * GROUP
 INFO = EDGE + 16
 MIB = 1024 * 1024
@@ -20,7 +22,7 @@
     return pltpu.CompilerParams(vmem_limit_bytes=mib * MIB)
 
 
-def pick_kernel(sec_ref, slab_ref, out_ref, held, sems):
+def pick_kernel(sec_ref, slab_ref, out_ref, held, turned, sems, out_sems):
     sec = sec_ref[0]
     copies = []
     for x in range(4):
@@ -34,11 +36,17 @@
     chosen = jnp.where(lane == wanted, 1.0, 0.0).astype(jnp.bfloat16)
     for x in range(4):
         copies[x].wait()
-        turned = lax.dot_general(
+        turned[x] = lax.dot_general(
             chosen, held[x], (((1,), (1,)), ((), ())), preferred_element_type=jnp.float32
         ).astype(jnp.bfloat16)
         for quarter in range(QUARTERS):
-            out_ref[x * QUARTERS + quarter] = turned
+            place_at = x * QUARTERS + quarter
+            copies.append(
+                pltpu.make_async_copy(turned.at[x], out_ref.at[place_at], out_sems.at[place_at])
+            )
+            copies[-1].start()
+    for copy in copies[4:]:
+        copy.wait()
 
 
 def pick(sec, slab_rows):
@@ -46,96 +54,107 @@
     return pl.pallas_call(
         pick_kernel,
         in_specs=[pl.BlockSpec(memory_space=pltpu.SMEM), pl.BlockSpec(memory_space=pl.ANY)],
-        out_specs=pl.BlockSpec(memory_space=pltpu.VMEM),
+        out_specs=pl.BlockSpec(memory_space=pl.ANY),
         out_shape=jax.ShapeDtypeStruct((4 * QUARTERS, SPAN // 2, length), jnp.bfloat16),
-        scratch_shapes=[pltpu.VMEM((4, length, SPAN), jnp.bfloat16), pltpu.SemaphoreType.DMA((4,))],
+        scratch_shapes=[
+            pltpu.VMEM((4, length, SPAN), jnp.bfloat16),
+            pltpu.VMEM((4, SPAN // 2, length), jnp.bfloat16),
+            pltpu.SemaphoreType.DMA((4,)),
+            pltpu.SemaphoreType.DMA((4 * QUARTERS,)),
+        ],
         name="pick",
     )(sec, slab_rows)
 
 
-def chain_kernel(where_ref, x_ref, par_ref, out_ref, kept_ref, par, y_ref, sems, kept_sems):
+def section_params(step, sec, quarter, par):
+    lane = lax.broadcasted_iota(jnp.int32, (GROUP, TAPS), 1)
+    chan = lax.broadcasted_iota(jnp.int32, (GROUP, TAPS), 0)
+    slot = 2 * ((step // 2) ^ quarter) + ((step % 2) ^ (sec % 2))
+    skip_row = jnp.broadcast_to(par[pl.ds(slot * 8 + 4, 1), :], (GROUP, TAPS))
+    bands, gains = [], []
+    for part in range(WIDE // GROUP):
+        taps_row = par[pl.ds(slot * 8 + 2 * (sec % 2) + part, 1), :]
+        spread = jnp.concatenate([taps_row, jnp.zeros_like(taps_row)], axis=1)
+        spread = jnp.broadcast_to(spread, (TAPS, 2 * TAPS))
+        bands.append(pltpu.roll(spread, 0, 1, stride=1, stride_axis=0).astype(jnp.bfloat16))
+        own = jnp.where(lane == (sec % 2) * WIDE + part * GROUP + chan, skip_row, 0.0)
+        gains.append(jnp.broadcast_to(jnp.sum(own, axis=1, keepdims=True), (GROUP, TAPS)))
+    return bands, gains
+
+
+def serve_kernel(where_ref, x_ref, par_ref, out_ref, par, state, sems):
     sec = where_ref[0]
     quarter = where_ref[1]
     sections = out_ref.shape[0]
-    blocks = x_ref.shape[0]
-    share = 16
+    reach = HALO + SERVED
     par[...] = par_ref[...].astype(jnp.float32)
-    lane = lax.broadcasted_iota(jnp.int32, (GROUP, TAPS), 1)
-    chan = lax.broadcasted_iota(jnp.int32, (GROUP, TAPS), 0)
+
+    for ahead in range(HALO // SERVED):
+
+        @pl.when(quarter == ahead)
+        def _():
+            missing = HALO - SERVED * ahead
+            state[0, 0, :missing] = jnp.zeros((missing, WIDE, TAPS), jnp.bfloat16)
+            state[0, 0, missing:] = x_ref[: reach - missing]
+
+    @pl.when(quarter >= HALO // SERVED)
+    def _():
+        state[0, 0] = x_ref[pl.ds(SERVED * quarter - HALO, reach)]
+
+    for x in range(1, 4):
+        state[0, x] = x_ref[pl.ds(16 * x + SERVED * quarter - HALO, reach)]
+
     copies = []
     for step in range(sections):
-        slot = (step // 2) ^ quarter
-        slot = 2 * slot + ((step % 2) ^ (sec % 2))
-
-        def source(first, last, low):
-            if step == 0:
-                return x_ref[first:last, low : low + GROUP, :]
-            return y_ref[step - 1, first:last, low : low + GROUP, :]
-
-        skip_row = jnp.broadcast_to(par[pl.ds(slot * 8 + 4, 1), :], (GROUP, TAPS))
-        for part in range(WIDE // GROUP):
-            low = part * GROUP
-            taps_row = par[pl.ds(slot * 8 + 2 * (sec % 2) + part, 1), :]
-            spread = jnp.concatenate([taps_row, jnp.zeros_like(taps_row)], axis=1)
-            spread = jnp.broadcast_to(spread, (TAPS, 2 * TAPS))
-            band = pltpu.roll(spread, 0, 1, stride=1, stride_axis=0).astype(jnp.bfloat16)
-            own = jnp.where(lane == (sec % 2) * WIDE + low + chan, skip_row, 0.0)
-            gain = jnp.broadcast_to(jnp.sum(own, axis=1, keepdims=True), (GROUP, TAPS))
-            carry = jnp.zeros((GROUP, TAPS), jnp.float32)
-            for first in range(0, blocks, share):
-                current = source(first, first + share, low).reshape(share * GROUP, TAPS)
-                both = jnp.dot(current, band, preferred_element_type=jnp.float32)
-                carried = jnp.concatenate([carry, both[: (share - 1) * GROUP, TAPS:]], axis=0)
-                carry = both[(share - 1) * GROUP :, TAPS:]
-                direct = current.astype(jnp.float32).reshape(share, GROUP, TAPS) * gain[None]
-                filtered = both[:, :TAPS] + carried + direct.reshape(share * GROUP, TAPS)
-                y_ref[step, first : first + share, low : low + GROUP, :] = filtered.astype(
+        bands, gains = section_params(step, sec, quarter, par)
+        count = reach - step
+        for x in range(4):
+            for part in range(WIDE // GROUP):
+                low = part * GROUP
+                current = state[step, x, step:, low : low + GROUP, :].reshape(count * GROUP, TAPS)
+                both = jnp.dot(current, bands[part], preferred_element_type=jnp.float32)
+                direct = current[GROUP:].astype(jnp.float32).reshape(count - 1, GROUP, TAPS)
+                direct = (direct * gains[part][None]).reshape((count - 1) * GROUP, TAPS)
+                filtered = both[GROUP:, :TAPS] + both[:-GROUP, TAPS:] + direct
+                state[step + 1, x, step + 1 :, low : low + GROUP, :] = filtered.astype(
                     jnp.bfloat16
-                ).reshape(share, GROUP, TAPS)
-        for x in range(4):
-            begin = 16 * x + 4 * quarter
+                ).reshape(count - 1, GROUP, TAPS)
             copies.append(
                 pltpu.make_async_copy(
-                    y_ref.at[step, pl.ds(begin, 4)], out_ref.at[step, x], sems.at[step, x]
+                    state.at[step + 1, x, pl.ds(HALO, SERVED)], out_ref.at[step, x], sems.at[step, x]
                 )
-            )
-            copies[-1].start()
-        if step + 1 < sections:
-            copies.append(
-                pltpu.make_async_copy(y_ref.at[step], kept_ref.at[step], kept_sems.at[step])
             )
             copies[-1].start()
     for copy in copies:
         copy.wait()
 
 
-def chain(where, rows_in, params, sections):
-    blocks = rows_in.shape[0]
+def serve(where, rows_in, params, sections):
     return pl.pallas_call(
-        chain_kernel,
+        serve_kernel,
         in_specs=[pl.BlockSpec(memory_space=pltpu.SMEM)] + [pl.BlockSpec(memory_space=pltpu.VMEM)] * 2,
-        out_specs=[pl.BlockSpec(memory_space=pl.ANY)] * 2,
-        out_shape=[
-            jax.ShapeDtypeStruct((sections, 4, 4, WIDE, TAPS), jnp.bfloat16),
-            pltpu.HBM((sections - 1, blocks, WIDE, TAPS), jnp.bfloat16),
-        ],
+        out_specs=pl.BlockSpec(memory_space=pl.ANY),
+        out_shape=jax.ShapeDtypeStruct((sections, 4, SERVED, WIDE, TAPS), jnp.bfloat16),
         scratch_shapes=[
             pltpu.VMEM(params.shape, jnp.float32),
-            pltpu.VMEM((sections, blocks, WIDE, TAPS), jnp.bfloat16),
+            pltpu.VMEM((sections + 1, 4, HALO + SERVED, WIDE, TAPS), jnp.bfloat16),
             pltpu.SemaphoreType.DMA((sections, 4)),
-            pltpu.SemaphoreType.DMA((sections - 1,)),
         ],
         compiler_params=limits(24),
-        name="chain",
+        name="serve",
     )(where, rows_in, params)
 
 
-def lags_kernel(where_ref, x_ref, y_ref, info_ref):
+def lags_kernel(where_ref, x_ref, par_ref, info_ref, par, y_ref):
+    sec = where_ref[0]
     quarter = where_ref[1]
+    share = 16
     sections, blocks = y_ref.shape[0] + 1, y_ref.shape[1]
     rows = (blocks - 1) * GROUP
     blank = jnp.zeros((GROUP, TAPS), jnp.bfloat16)
+    par[...] = par_ref[...].astype(jnp.float32)
     for step in range(sections):
+        bands, gains = section_params(step, sec, quarter, par)
         slot = (step // 2) ^ quarter
         for part in range(WIDE // GROUP):
             low = part * GROUP
@@ -143,6 +162,17 @@
                 whole = x_ref[:, low : low + GROUP, :]
             else:
                 whole = y_ref[step - 1, :, low : low + GROUP, :]
+            carry = jnp.zeros((GROUP, TAPS), jnp.float32)
+            for first in range(0, blocks if step + 1 < sections else 0, share):
+                current = whole[first : first + share].reshape(share * GROUP, TAPS)
+                both = jnp.dot(current, bands[part], preferred_element_type=jnp.float32)
+                carried = jnp.concatenate([carry, both[: (share - 1) * GROUP, TAPS:]], axis=0)
+                carry = both[(share - 1) * GROUP :, TAPS:]
+                direct = current.astype(jnp.float32).reshape(share, GROUP, TAPS) * gains[part][None]
+                filtered = both[:, :TAPS] + carried + direct.reshape(share * GROUP, TAPS)
+                y_ref[step, first : first + share, low : low + GROUP, :] = filtered.astype(
+                    jnp.bfloat16
+                ).reshape(share, GROUP, TAPS)
             body = whole[: blocks - 1].reshape(rows, TAPS)
             after = jnp.concatenate([body[GROUP:], blank], axis=0)
             pair = jnp.concatenate([body, after], axis=1)
@@ -171,19 +201,25 @@
             info_ref[slot, step % 2, part] = piece
 
 
-def lag_info(where, rows_in, states):
-    sections = states.shape[0] + 1
+def lag_info(where, rows_in, params, sections):
+    blocks = rows_in.shape[0]
     return pl.pallas_call(
         lags_kernel,
         in_specs=[pl.BlockSpec(memory_space=pltpu.SMEM)] + [pl.BlockSpec(memory_space=pltpu.VMEM)] * 2,
         out_specs=pl.BlockSpec(memory_space=pltpu.VMEM),
         out_shape=jax.ShapeDtypeStruct((sections // 2, 2, WIDE // GROUP, INFO, TAPS), jnp.bfloat16),
-        compiler_params=limits(16),
+        scratch_shapes=[
+            pltpu.VMEM(params.shape, jnp.float32),
+            pltpu.VMEM((sections - 1, blocks, WIDE, TAPS), jnp.bfloat16),
+        ],
+        compiler_params=limits(24),
         cost_estimate=pl.CostEstimate(
-            flops=4 * states.size * TAPS, bytes_accessed=2 * states.size, transcendentals=0
+            flops=8 * sections * rows_in.size * TAPS,
+            bytes_accessed=4 * sections * rows_in.size,
+            transcendentals=0,
         ),
         name="lags",
-    )(where, rows_in, states)
+    )(where, rows_in, params)
 
 
 def place_kernel(x_ref, out_ref, turned, sems):
@@ -272,7 +308,7 @@
     moved = lax.all_to_all(
         picked.reshape(64, WIDE, TAPS), ("x", "quarter", "slot"), split_axis=0, concat_axis=0, tiled=True
     )
-    outputs, states = chain(where, moved, params, sections)
+    outputs = serve(where, moved, params, sections)
     pieces = lax.all_to_all(
         outputs.reshape(sections * 16, WIDE, TAPS),
         ("section", "x", "slot"),
@@ -281,7 +317,7 @@
         tiled=True,
     )
 
-    info = lag_info(where, moved, states)
+    info = lag_info(where, moved, params, sections)
     local = jnp.where(section // 2 == quarter, info[0], jnp.zeros_like(info[0]))
     info = local + home_round(info[1], 1) + home_round(info[2], 2) + home_round(info[3], 3)
     odd = (section & 1) != 0

time: 101 us -> 100 us (0.990)
  waiting for transfers between devices: 22.8 us -> 24.6 us
  other arithmetic: 2.75 us -> 1.35 us
  local copies, waits for them, and re-layouts: 3.72 us -> 2.36 us
    unnamed x5 -> x7, local copies, waits for them, and re-layouts: 2.06 us -> 0.7 us
    all_to_all x1, waiting for transfers between devices: 6.02 us -> 7.15 us  [per_device(): lax.all_to_all(outputs.reshape(sections * 16, WIDE, TAPS), ('section', 'x...]
    pallas_call x1, Pallas kernels: 5.74 us -> 6.79 us  [lag_info(): pl.pallas_call(lags_kernel, in_specs=[pl.BlockSpec(memory_space=pltpu.SME...]
  transfers between devices with their start and end apart: 11 -> 11, of which waited for: 6 -> 6; matrix products, arithmetic and copies ran while one was open for 5% -> 3% of each run, Pallas kernels for 6% -> 7%
where the time goes in v4:
time: 100 us; the launch traced here: 99.6 us
  starting transfers between devices  56.7 us (57%)
  waiting for transfers between devices  24.6 us (25%)
  Pallas kernels  13.3 us (13%)
  local copies, waits for them, and re-layouts  2.36 us (2%)
  other arithmetic  1.35 us (1%)
  between operations  1 us (1%)
    all_to_all x1, starting transfers between devices, per_device(): lax.all_to_all(picked.reshape(64, WIDE, TAPS), ('x', 'quarter', 'slot'),...  19.1 us
    all_to_all x1, starting transfers between devices, per_device(): lax.all_to_all(outputs.reshape(sections * 16, WIDE, TAPS), ('section', 'x...  14.3 us
    all_to_all x1, waiting for transfers between devices, per_device(): lax.all_to_all(picked.reshape(64, WIDE, TAPS), ('x', 'quarter', 'slot'),...  10.8 us
    ppermute x3, starting transfers between devices, per_device(): lax.ppermute(params, 'section', [(i, i ^ 2 * offset) for i in range(8)])  9.64 us
    all_to_all x1, waiting for transfers between devices, per_device(): lax.all_to_all(outputs.reshape(sections * 16, WIDE, TAPS), ('section', 'x...  7.15 us
    ppermute x3, starting transfers between devices, home_round(): return lax.ppermute(value, EVERY, pairs)  7.14 us
    pallas_call x1, Pallas kernels, lag_info(): pl.pallas_call(lags_kernel, in_specs=[pl.BlockSpec(memory_space=pltpu.SME...  6.79 us
    ppermute x2, starting transfers between devices, swap_cores(): return lax.ppermute(value, 'section', [(i, i ^ 1) for i in range(8)])  5.79 us
  transfers between devices with their start and end apart: 11, of which 6 were waited for; matrix products, arithmetic and copies ran while one was open for 3% of the time, Pallas kernels for 7%

profile of v4, /device:TPU:1, one launch (start us, length us, event | category | flops | bytes accessed | tf_op | source)
XLA Modules:
  0.0 99.6 jit_solution(15599252298941787161)
XLA Ops:
  0.6 2.4 %pick.1 = bf16[16,128,128]{2,1,0:T(8,128)(2,1)} custom-call(s32[1]{0:T(128)} %bitcast.sec_ref, bf16[128,4096]{1,0:T(8,128)(2,1)} %slab_ref.1), custom_call_target="tpu_custom_call" | custom-call | tf_op jit(solution)/shard_map/pick/pallas_call | solution.py:54
  3.1 19.1 %all-to-all-start = ((bf16[64,32,128]{2,1,0:T(8,128)(2,1)}), bf16[64,32,128]{2,1,0:T(8,128)(2,1)S(1)}, u32[]{:S(2)}, u32[]{:S(2)}) async-start(bf16[64,32,128]{2,1,0:T(8,128)(2,1)} %bitcast.42), calls=%async_computation | async-start | bytes 1048576 | tf_op jit(solution)/shard_map/all_to_all | solution.py:308
  22.2 0.7 copy-done
  22.9 2.9 %collective-permute-start = (bf16[1,8,128]{2,1,0:T(8,128)(2,1)S(1)}, bf16[1,8,128]{2,1,0:T(8,128)(2,1)S(1)}, u32[]{:S(2)}, u32[]{:S(2)}) collective-permute-start(bf16[1,8,128]{2,1,0:T(8,128)(2,1)S(1)} %fusion.11), channel_id=1, source_target_pairs={{0,64},{64,0},{128,192},{192,128},{256,320},{320,256},{384,448},{4... | collective-permute-start | bytes 6152 | tf_op jit(solution)/shard_map/ppermute | solution.py:286
  25.8 0.8 collective-permute-done
  26.5 3.2 %collective-permute-start.1 = (bf16[2,8,128]{2,1,0:T(8,128)(2,1)S(1)}, bf16[2,8,128]{2,1,0:T(8,128)(2,1)S(1)}, u32[]{:S(2)}, u32[]{:S(2)}) collective-permute-start(bf16[2,8,128]{2,1,0:T(8,128)(2,1)S(1)} %pad_maximum_fusion), channel_id=1, source_target_pairs={{0,128},{64,192},{128,0},{192,64},{256,384},{320,448},{384,256},{4... | collective-permute-start | bytes 12296 | tf_op jit(solution)/shard_map/ppermute | solution.py:301
  29.7 4.5 %collective-permute-start.2 = (bf16[2,8,128]{2,1,0:T(8,128)(2,1)S(1)}, bf16[2,8,128]{2,1,0:T(8,128)(2,1)S(1)}, u32[]{:S(2)}, u32[]{:S(2)}) collective-permute-start(bf16[2,8,128]{2,1,0:T(8,128)(2,1)S(1)} %pad_maximum_fusion), channel_id=1, source_target_pairs={{0,256},{64,320},{128,384},{192,448},{256,0},{320,64},{384,128},{4... | collective-permute-start | bytes 12296 | tf_op jit(solution)/shard_map/ppermute | solution.py:301
  34.3 1.9 %collective-permute-start.3 = (bf16[2,8,128]{2,1,0:T(8,128)(2,1)S(1)}, bf16[2,8,128]{2,1,0:T(8,128)(2,1)S(1)}, u32[]{:S(2)}, u32[]{:S(2)}) collective-permute-start(bf16[2,8,128]{2,1,0:T(8,128)(2,1)S(1)} %pad_maximum_fusion), channel_id=1, source_target_pairs={{0,384},{64,448},{128,256},{192,320},{256,128},{320,192},{384,0},{... | collective-permute-start | bytes 12296 | tf_op jit(solution)/shard_map/ppermute | solution.py:301
  36.3 3.9 %collective-permute-done.3 = bf16[2,8,128]{2,1,0:T(8,128)(2,1)S(1)} collective-permute-done((bf16[2,8,128]{2,1,0:T(8,128)(2,1)S(1)}, bf16[2,8,128]{2,1,0:T(8,128)(2,1)S(1)}, u32[]{:S(2)}, u32[]{:S(2)}) %collective-permute-start.3) | collective-permute-done | bytes 4128 | tf_op jit(solution)/shard_map/ppermute | solution.py:301
  40.1 0.7 collective-permute-start.4
  40.9 10.8 %all-to-all-done.x_ref = bf16[64,32,128]{2,1,0:T(8,128)(2,1)S(1)} async-done(((bf16[64,32,128]{2,1,0:T(8,128)(2,1)}), bf16[64,32,128]{2,1,0:T(8,128)(2,1)S(1)}, u32[]{:S(2)}, u32[]{:S(2)}) %all-to-all-start) | async-done | bytes 524320 | tf_op jit(solution)/shard_map/all_to_all | solution.py:308
  51.7 3.0 %serve.1 = bf16[8,4,4,32,128]{4,3,2,1,0:T(8,128)(2,1)} custom-call(s32[2]{0:T(128)S(1)} %pad_add_fusion.7.where_ref, bf16[64,32,128]{2,1,0:T(8,128)(2,1)S(1)} %all-to-all-done.x_ref, bf16[64,128]{1,0:T(8,128)(2,1)S(1)} %bitcast.40), custom_call_target="tpu_custom_call" | custom-call | tf_op jit(solution)/shard_map/serve/pallas_call | solution.py:133
  54.7 14.3 %all-to-all-start.1 = ((bf16[128,32,128]{2,1,0:T(8,128)(2,1)}), bf16[128,32,128]{2,1,0:T(8,128)(2,1)S(1)}, u32[]{:S(2)}, u32[]{:S(2)}) async-start(bf16[128,32,128]{2,1,0:T(8,128)(2,1)} %bitcast.6), calls=%async_computation.1 | async-start | bytes 2097152 | tf_op jit(solution)/shard_map/all_to_all | solution.py:312
  69.1 6.8 %lags.1 = bf16[4,2,2,48,128]{4,3,2,1,0:T(8,128)(2,1)S(1)} custom-call(s32[2]{0:T(128)S(1)} %pad_add_fusion.7.where_ref, bf16[64,32,128]{2,1,0:T(8,128)(2,1)S(1)} %all-to-all-done.x_ref, bf16[64,128]{1,0:T(8,128)(2,1)S(1)} %bitcast.41), custom_call_target="tpu_custom_call" | custom-call | flops 2147483648 | bytes 8388608 | tf_op jit(solution)/shard_map/lags/pallas_call | solution.py:206
  75.9 3.5 %collective-permute-start.5 = (bf16[2,2,48,128]{3,2,1,0:T(8,128)(2,1)S(1)}, bf16[2,2,48,128]{3,2,1,0:T(8,128)(2,1)S(1)}, u32[]{:S(2)}, u32[]{:S(2)}) collective-permute-start(bf16[2,2,48,128]{3,2,1,0:T(8,128)(2,1)S(1)} %get-tuple-element.2), channel_id=1, source_target_pairs={{0,128},{64,192},{132,4},{196,68},{264,392},{328,456},{396,268},{4... | collective-permute-start | bytes 147464 | tf_op jit(solution)/shard_map/ppermute | solution.py:282
  79.3 2.4 %collective-permute-start.6 = (bf16[2,2,48,128]{3,2,1,0:T(8,128)(2,1)S(1)}, bf16[2,2,48,128]{3,2,1,0:T(8,128)(2,1)S(1)}, u32[]{:S(2)}, u32[]{:S(2)}) collective-permute-start(bf16[2,2,48,128]{3,2,1,0:T(8,128)(2,1)S(1)} %get-tuple-element.4), channel_id=1, source_target_pairs={{0,256},{64,320},{132,388},{196,452},{264,8},{328,72},{396,140},{4... | collective-permute-start | bytes 147464 | tf_op jit(solution)/shard_map/ppermute | solution.py:282
  81.7 1.3 %collective-permute-start.7 = (bf16[2,2,48,128]{3,2,1,0:T(8,128)(2,1)S(1)}, bf16[2,2,48,128]{3,2,1,0:T(8,128)(2,1)S(1)}, u32[]{:S(2)}, u32[]{:S(2)}) collective-permute-start(bf16[2,2,48,128]{3,2,1,0:T(8,128)(2,1)S(1)} %get-tuple-element.3), channel_id=1, source_target_pairs={{0,384},{64,448},{132,260},{196,324},{264,136},{328,200},{396,12},... | collective-permute-start | bytes 147464 | tf_op jit(solution)/shard_map/ppermute | solution.py:282
  83.1 1.2 %collective-permute-done.7 = bf16[2,2,48,128]{3,2,1,0:T(8,128)(2,1)S(1)} collective-permute-done((bf16[2,2,48,128]{3,2,1,0:T(8,128)(2,1)S(1)}, bf16[2,2,48,128]{3,2,1,0:T(8,128)(2,1)S(1)}, u32[]{:S(2)}, u32[]{:S(2)}) %collective-permute-start.7) | collective-permute-done | bytes 49184 | tf_op jit(solution)/shard_map/ppermute | solution.py:282
  84.4 2.9 %collective-permute-start.8 = (bf16[2,48,128]{2,1,0:T(8,128)(2,1)S(1)}, bf16[2,48,128]{2,1,0:T(8,128)(2,1)S(1)}, u32[]{:S(2)}, u32[]{:S(2)}) collective-permute-start(bf16[2,48,128]{2,1,0:T(8,128)(2,1)S(1)} %get-tuple-element.7), channel_id=1, source_target_pairs={{0,64},{64,0},{128,192},{192,128},{256,320},{320,256},{384,448},{4... | collective-permute-start | bytes 73736 | tf_op jit(solution)/shard_map/ppermute | solution.py:286
  87.3 0.8 collective-permute-done.8
  88.4 0.3 convolution_add_fusion
  88.7 0.2 slice.79
  89.0 0.2 slice.80
  89.3 0.2 slice.81
  89.6 0.2 slice.82
  89.8 0.2 slice.83
  90.1 0.2 slice.84
  90.3 0.1 slice.85
  90.5 0.1 copy.5
  90.6 0.7 fusion.1
  91.4 7.1 %all-to-all-done.1 = bf16[128,32,128]{2,1,0:T(8,128)(2,1)S(1)} async-done(((bf16[128,32,128]{2,1,0:T(8,128)(2,1)}), bf16[128,32,128]{2,1,0:T(8,128)(2,1)S(1)}, u32[]{:S(2)}, u32[]{:S(2)}) %all-to-all-start.1) | async-done | bytes 1048608 | tf_op jit(solution)/shard_map/all_to_all | solution.py:312
  98.5 1.1 %place.1 = bf16[128,4096]{1,0:T(8,128)(2,1)} custom-call(bf16[8,4,4,32,128]{4,3,2,1,0:T(8,128)(2,1)S(1)} %bitcast.39), custom_call_target="tpu_custom_call" | custom-call | tf_op jit(solution)/shard_map/place/pallas_call | solution.py:247
  (34 shorter events, 0.9 us)
Async XLA Ops:
  3.1 48.6 %all-to-all-start = ((bf16[64,32,128]{2,1,0:T(8,128)(2,1)}), bf16[64,32,128]{2,1,0:T(8,128)(2,1)S(1)}, u32[]{:S(2)}, u32[]{:S(2)}) async-start(bf16[64,32,128]{2,1,0:T(8,128)(2,1)} %bitcast.42), calls=%async_computation | async-start | bytes 1048576 | tf_op jit(solution)/shard_map/all_to_all | solution.py:308
  22.2 0.7 copy-start
  22.2 0.7 copy-start.1
  22.9 3.7 %collective-permute-start = (bf16[1,8,128]{2,1,0:T(8,128)(2,1)S(1)}, bf16[1,8,128]{2,1,0:T(8,128)(2,1)S(1)}, u32[]{:S(2)}, u32[]{:S(2)}) collective-permute-start(bf16[1,8,128]{2,1,0:T(8,128)(2,1)S(1)} %fusion.11), channel_id=1, source_target_pairs={{0,64},{64,0},{128,192},{192,128},{256,320},{320,256},{384,448},{4... | collective-permute-start | bytes 6152 | tf_op jit(solution)/shard_map/ppermute | solution.py:286
  26.5 9.7 %collective-permute-start.1 = (bf16[2,8,128]{2,1,0:T(8,128)(2,1)S(1)}, bf16[2,8,128]{2,1,0:T(8,128)(2,1)S(1)}, u32[]{:S(2)}, u32[]{:S(2)}) collective-permute-start(bf16[2,8,128]{2,1,0:T(8,128)(2,1)S(1)} %pad_maximum_fusion), channel_id=1, source_target_pairs={{0,128},{64,192},{128,0},{192,64},{256,384},{320,448},{384,256},{4... | collective-permute-start | bytes 12296 | tf_op jit(solution)/shard_map/ppermute | solution.py:301
  29.7 6.5 %collective-permute-start.2 = (bf16[2,8,128]{2,1,0:T(8,128)(2,1)S(1)}, bf16[2,8,128]{2,1,0:T(8,128)(2,1)S(1)}, u32[]{:S(2)}, u32[]{:S(2)}) collective-permute-start(bf16[2,8,128]{2,1,0:T(8,128)(2,1)S(1)} %pad_maximum_fusion), channel_id=1, source_target_pairs={{0,256},{64,320},{128,384},{192,448},{256,0},{320,64},{384,128},{4... | collective-permute-start | bytes 12296 | tf_op jit(solution)/shard_map/ppermute | solution.py:301
  34.3 5.9 %collective-permute-start.3 = (bf16[2,8,128]{2,1,0:T(8,128)(2,1)S(1)}, bf16[2,8,128]{2,1,0:T(8,128)(2,1)S(1)}, u32[]{:S(2)}, u32[]{:S(2)}) collective-permute-start(bf16[2,8,128]{2,1,0:T(8,128)(2,1)S(1)} %pad_maximum_fusion), channel_id=1, source_target_pairs={{0,384},{64,448},{128,256},{192,320},{256,128},{320,192},{384,0},{... | collective-permute-start | bytes 12296 | tf_op jit(solution)/shard_map/ppermute | solution.py:301
  40.1 0.7 collective-permute-start.4
  54.7 43.8 %all-to-all-start.1 = ((bf16[128,32,128]{2,1,0:T(8,128)(2,1)}), bf16[128,32,128]{2,1,0:T(8,128)(2,1)S(1)}, u32[]{:S(2)}, u32[]{:S(2)}) async-start(bf16[128,32,128]{2,1,0:T(8,128)(2,1)} %bitcast.6), calls=%async_computation.1 | async-start | bytes 2097152 | tf_op jit(solution)/shard_map/all_to_all | solution.py:312
  75.9 7.2 %collective-permute-start.5 = (bf16[2,2,48,128]{3,2,1,0:T(8,128)(2,1)S(1)}, bf16[2,2,48,128]{3,2,1,0:T(8,128)(2,1)S(1)}, u32[]{:S(2)}, u32[]{:S(2)}) collective-permute-start(bf16[2,2,48,128]{3,2,1,0:T(8,128)(2,1)S(1)} %get-tuple-element.2), channel_id=1, source_target_pairs={{0,128},{64,192},{132,4},{196,68},{264,392},{328,456},{396,268},{4... | collective-permute-start | bytes 147464 | tf_op jit(solution)/shard_map/ppermute | solution.py:282
  79.3 3.7 %collective-permute-start.6 = (bf16[2,2,48,128]{3,2,1,0:T(8,128)(2,1)S(1)}, bf16[2,2,48,128]{3,2,1,0:T(8,128)(2,1)S(1)}, u32[]{:S(2)}, u32[]{:S(2)}) collective-permute-start(bf16[2,2,48,128]{3,2,1,0:T(8,128)(2,1)S(1)} %get-tuple-element.4), channel_id=1, source_target_pairs={{0,256},{64,320},{132,388},{196,452},{264,8},{328,72},{396,140},{4... | collective-permute-start | bytes 147464 | tf_op jit(solution)/shard_map/ppermute | solution.py:282
  81.7 2.6 %collective-permute-start.7 = (bf16[2,2,48,128]{3,2,1,0:T(8,128)(2,1)S(1)}, bf16[2,2,48,128]{3,2,1,0:T(8,128)(2,1)S(1)}, u32[]{:S(2)}, u32[]{:S(2)}) collective-permute-start(bf16[2,2,48,128]{3,2,1,0:T(8,128)(2,1)S(1)} %get-tuple-element.3), channel_id=1, source_target_pairs={{0,384},{64,448},{132,260},{196,324},{264,136},{328,200},{396,12},... | collective-permute-start | bytes 147464 | tf_op jit(solution)/shard_map/ppermute | solution.py:282
  84.4 3.8 %collective-permute-start.8 = (bf16[2,48,128]{2,1,0:T(8,128)(2,1)S(1)}, bf16[2,48,128]{2,1,0:T(8,128)(2,1)S(1)}, u32[]{:S(2)}, u32[]{:S(2)}) collective-permute-start(bf16[2,48,128]{2,1,0:T(8,128)(2,1)S(1)} %get-tuple-element.7), channel_id=1, source_target_pairs={{0,64},{64,0},{128,192},{192,128},{256,320},{320,256},{384,448},{4... | collective-permute-start | bytes 73736 | tf_op jit(solution)/shard_map/ppermute | solution.py:286

commit v5 on v4

--- a/solution.py
+++ b/solution.py
@@ -108,23 +108,21 @@
     for step in range(sections):
         bands, gains = section_params(step, sec, quarter, par)
         count = reach - step
-        for x in range(4):
-            for part in range(WIDE // GROUP):
-                low = part * GROUP
-                current = state[step, x, step:, low : low + GROUP, :].reshape(count * GROUP, TAPS)
-                both = jnp.dot(current, bands[part], preferred_element_type=jnp.float32)
-                direct = current[GROUP:].astype(jnp.float32).reshape(count - 1, GROUP, TAPS)
-                direct = (direct * gains[part][None]).reshape((count - 1) * GROUP, TAPS)
-                filtered = both[GROUP:, :TAPS] + both[:-GROUP, TAPS:] + direct
-                state[step + 1, x, step + 1 :, low : low + GROUP, :] = filtered.astype(
-                    jnp.bfloat16
-                ).reshape(count - 1, GROUP, TAPS)
-            copies.append(
-                pltpu.make_async_copy(
-                    state.at[step + 1, x, pl.ds(HALO, SERVED)], out_ref.at[step, x], sems.at[step, x]
-                )
+        for part in range(WIDE // GROUP):
+            low = part * GROUP
+            current = state[step, :, step:, low : low + GROUP, :]
+            both = jnp.dot(
+                current.reshape(4 * count * GROUP, TAPS), bands[part], preferred_element_type=jnp.float32
+            ).reshape(4, count, GROUP, 2 * TAPS)
+            direct = current[:, 1:].astype(jnp.float32) * gains[part][None, None]
+            filtered = both[:, 1:, :, :TAPS] + both[:, :-1, :, TAPS:] + direct
+            state[step + 1, :, step + 1 :, low : low + GROUP, :] = filtered.astype(jnp.bfloat16)
+        copies.append(
+            pltpu.make_async_copy(
+                state.at[step + 1, :, pl.ds(HALO, SERVED)], out_ref.at[step], sems.at[step]
             )
-            copies[-1].start()
+        )
+        copies[-1].start()
     for copy in copies:
         copy.wait()
 
@@ -138,7 +136,7 @@
         scratch_shapes=[
             pltpu.VMEM(params.shape, jnp.float32),
             pltpu.VMEM((sections + 1, 4, HALO + SERVED, WIDE, TAPS), jnp.bfloat16),
-            pltpu.SemaphoreType.DMA((sections, 4)),
+            pltpu.SemaphoreType.DMA((sections,)),
         ],
         compiler_params=limits(24),
         name="serve",

time: 100 us -> 100 us (level)
  no operation moved by 1% of the time
where the time goes in v5:
time: 100 us; the launch traced here: 99.5 us
  starting transfers between devices  56.7 us (57%)
  waiting for transfers between devices  24.6 us (25%)
  Pallas kernels  13.2 us (13%)
  local copies, waits for them, and re-layouts  2.36 us (2%)
  other arithmetic  1.35 us (1%)
    all_to_all x1, starting transfers between devices, per_device(): lax.all_to_all(picked.reshape(64, WIDE, TAPS), ('x', 'quarter', 'slot'),...  19.1 us
    all_to_all x1, starting transfers between devices, per_device(): lax.all_to_all(outputs.reshape(sections * 16, WIDE, TAPS), ('section', 'x...  14.3 us
    all_to_all x1, waiting for transfers between devices, per_device(): lax.all_to_all(picked.reshape(64, WIDE, TAPS), ('x', 'quarter', 'slot'),...  10.8 us
    ppermute x3, starting transfers between devices, per_device(): lax.ppermute(params, 'section', [(i, i ^ 2 * offset) for i in range(8)])  9.64 us
    all_to_all x1, waiting for transfers between devices, per_device(): lax.all_to_all(outputs.reshape(sections * 16, WIDE, TAPS), ('section', 'x...  7.15 us
    ppermute x3, starting transfers between devices, home_round(): return lax.ppermute(value, EVERY, pairs)  7.14 us
    pallas_call x1, Pallas kernels, lag_info(): pl.pallas_call(lags_kernel, in_specs=[pl.BlockSpec(memory_space=pltpu.SME...  6.79 us
    ppermute x2, starting transfers between devices, swap_cores(): return lax.ppermute(value, 'section', [(i, i ^ 1) for i in range(8)])  5.79 us
  transfers between devices with their start and end apart: 11, of which 6 were waited for; matrix products, arithmetic and copies ran while one was open for 3% of the time, Pallas kernels for 7%

profile of v5, /device:TPU:1, one launch (start us, length us, event | category | flops | bytes accessed | tf_op | source)
XLA Modules:
  0.0 99.5 jit_solution(12669985445322889306)
XLA Ops:
  0.6 2.4 %pick.1 = bf16[16,128,128]{2,1,0:T(8,128)(2,1)} custom-call(s32[1]{0:T(128)} %bitcast.sec_ref, bf16[128,4096]{1,0:T(8,128)(2,1)} %slab_ref.1), custom_call_target="tpu_custom_call" | custom-call | tf_op jit(solution)/shard_map/pick/pallas_call | solution.py:54
  3.1 19.1 %all-to-all-start = ((bf16[64,32,128]{2,1,0:T(8,128)(2,1)}), bf16[64,32,128]{2,1,0:T(8,128)(2,1)S(1)}, u32[]{:S(2)}, u32[]{:S(2)}) async-start(bf16[64,32,128]{2,1,0:T(8,128)(2,1)} %bitcast.42), calls=%async_computation | async-start | bytes 1048576 | tf_op jit(solution)/shard_map/all_to_all | solution.py:306
  22.2 0.7 copy-done
  22.9 2.9 %collective-permute-start = (bf16[1,8,128]{2,1,0:T(8,128)(2,1)S(1)}, bf16[1,8,128]{2,1,0:T(8,128)(2,1)S(1)}, u32[]{:S(2)}, u32[]{:S(2)}) collective-permute-start(bf16[1,8,128]{2,1,0:T(8,128)(2,1)S(1)} %fusion.11), channel_id=1, source_target_pairs={{0,64},{64,0},{128,192},{192,128},{256,320},{320,256},{384,448},{4... | collective-permute-start | bytes 6152 | tf_op jit(solution)/shard_map/ppermute | solution.py:284
  25.8 0.8 collective-permute-done
  26.5 3.2 %collective-permute-start.1 = (bf16[2,8,128]{2,1,0:T(8,128)(2,1)S(1)}, bf16[2,8,128]{2,1,0:T(8,128)(2,1)S(1)}, u32[]{:S(2)}, u32[]{:S(2)}) collective-permute-start(bf16[2,8,128]{2,1,0:T(8,128)(2,1)S(1)} %pad_maximum_fusion), channel_id=1, source_target_pairs={{0,128},{64,192},{128,0},{192,64},{256,384},{320,448},{384,256},{4... | collective-permute-start | bytes 12296 | tf_op jit(solution)/shard_map/ppermute | solution.py:299
  29.7 4.5 %collective-permute-start.2 = (bf16[2,8,128]{2,1,0:T(8,128)(2,1)S(1)}, bf16[2,8,128]{2,1,0:T(8,128)(2,1)S(1)}, u32[]{:S(2)}, u32[]{:S(2)}) collective-permute-start(bf16[2,8,128]{2,1,0:T(8,128)(2,1)S(1)} %pad_maximum_fusion), channel_id=1, source_target_pairs={{0,256},{64,320},{128,384},{192,448},{256,0},{320,64},{384,128},{4... | collective-permute-start | bytes 12296 | tf_op jit(solution)/shard_map/ppermute | solution.py:299
  34.3 1.9 %collective-permute-start.3 = (bf16[2,8,128]{2,1,0:T(8,128)(2,1)S(1)}, bf16[2,8,128]{2,1,0:T(8,128)(2,1)S(1)}, u32[]{:S(2)}, u32[]{:S(2)}) collective-permute-start(bf16[2,8,128]{2,1,0:T(8,128)(2,1)S(1)} %pad_maximum_fusion), channel_id=1, source_target_pairs={{0,384},{64,448},{128,256},{192,320},{256,128},{320,192},{384,0},{... | collective-permute-start | bytes 12296 | tf_op jit(solution)/shard_map/ppermute | solution.py:299
  36.3 3.9 %collective-permute-done.3 = bf16[2,8,128]{2,1,0:T(8,128)(2,1)S(1)} collective-permute-done((bf16[2,8,128]{2,1,0:T(8,128)(2,1)S(1)}, bf16[2,8,128]{2,1,0:T(8,128)(2,1)S(1)}, u32[]{:S(2)}, u32[]{:S(2)}) %collective-permute-start.3) | collective-permute-done | bytes 4128 | tf_op jit(solution)/shard_map/ppermute | solution.py:299
  40.1 0.7 collective-permute-start.4
  40.9 10.8 %all-to-all-done.x_ref = bf16[64,32,128]{2,1,0:T(8,128)(2,1)S(1)} async-done(((bf16[64,32,128]{2,1,0:T(8,128)(2,1)}), bf16[64,32,128]{2,1,0:T(8,128)(2,1)S(1)}, u32[]{:S(2)}, u32[]{:S(2)}) %all-to-all-start) | async-done | bytes 524320 | tf_op jit(solution)/shard_map/all_to_all | solution.py:306
  51.7 2.9 %serve.1 = bf16[8,4,4,32,128]{4,3,2,1,0:T(8,128)(2,1)} custom-call(s32[2]{0:T(128)S(1)} %pad_add_fusion.7.where_ref, bf16[64,32,128]{2,1,0:T(8,128)(2,1)S(1)} %all-to-all-done.x_ref, bf16[64,128]{1,0:T(8,128)(2,1)S(1)} %bitcast.40), custom_call_target="tpu_custom_call" | custom-call | tf_op jit(solution)/shard_map/serve/pallas_call | solution.py:131
  54.6 14.3 %all-to-all-start.1 = ((bf16[128,32,128]{2,1,0:T(8,128)(2,1)}), bf16[128,32,128]{2,1,0:T(8,128)(2,1)S(1)}, u32[]{:S(2)}, u32[]{:S(2)}) async-start(bf16[128,32,128]{2,1,0:T(8,128)(2,1)} %bitcast.6), calls=%async_computation.1 | async-start | bytes 2097152 | tf_op jit(solution)/shard_map/all_to_all | solution.py:310
  68.9 6.8 %lags.1 = bf16[4,2,2,48,128]{4,3,2,1,0:T(8,128)(2,1)S(1)} custom-call(s32[2]{0:T(128)S(1)} %pad_add_fusion.7.where_ref, bf16[64,32,128]{2,1,0:T(8,128)(2,1)S(1)} %all-to-all-done.x_ref, bf16[64,128]{1,0:T(8,128)(2,1)S(1)} %bitcast.41), custom_call_target="tpu_custom_call" | custom-call | flops 2147483648 | bytes 8388608 | tf_op jit(solution)/shard_map/lags/pallas_call | solution.py:204
  75.7 3.5 %collective-permute-start.5 = (bf16[2,2,48,128]{3,2,1,0:T(8,128)(2,1)S(1)}, bf16[2,2,48,128]{3,2,1,0:T(8,128)(2,1)S(1)}, u32[]{:S(2)}, u32[]{:S(2)}) collective-permute-start(bf16[2,2,48,128]{3,2,1,0:T(8,128)(2,1)S(1)} %get-tuple-element.2), channel_id=1, source_target_pairs={{0,128},{64,192},{132,4},{196,68},{264,392},{328,456},{396,268},{4... | collective-permute-start | bytes 147464 | tf_op jit(solution)/shard_map/ppermute | solution.py:280
  79.2 2.4 %collective-permute-start.6 = (bf16[2,2,48,128]{3,2,1,0:T(8,128)(2,1)S(1)}, bf16[2,2,48,128]{3,2,1,0:T(8,128)(2,1)S(1)}, u32[]{:S(2)}, u32[]{:S(2)}) collective-permute-start(bf16[2,2,48,128]{3,2,1,0:T(8,128)(2,1)S(1)} %get-tuple-element.4), channel_id=1, source_target_pairs={{0,256},{64,320},{132,388},{196,452},{264,8},{328,72},{396,140},{4... | collective-permute-start | bytes 147464 | tf_op jit(solution)/shard_map/ppermute | solution.py:280
  81.6 1.3 %collective-permute-start.7 = (bf16[2,2,48,128]{3,2,1,0:T(8,128)(2,1)S(1)}, bf16[2,2,48,128]{3,2,1,0:T(8,128)(2,1)S(1)}, u32[]{:S(2)}, u32[]{:S(2)}) collective-permute-start(bf16[2,2,48,128]{3,2,1,0:T(8,128)(2,1)S(1)} %get-tuple-element.3), channel_id=1, source_target_pairs={{0,384},{64,448},{132,260},{196,324},{264,136},{328,200},{396,12},... | collective-permute-start | bytes 147464 | tf_op jit(solution)/shard_map/ppermute | solution.py:280
  82.9 1.2 %collective-permute-done.7 = bf16[2,2,48,128]{3,2,1,0:T(8,128)(2,1)S(1)} collective-permute-done((bf16[2,2,48,128]{3,2,1,0:T(8,128)(2,1)S(1)}, bf16[2,2,48,128]{3,2,1,0:T(8,128)(2,1)S(1)}, u32[]{:S(2)}, u32[]{:S(2)}) %collective-permute-start.7) | collective-permute-done | bytes 49184 | tf_op jit(solution)/shard_map/ppermute | solution.py:280
  84.2 2.9 %collective-permute-start.8 = (bf16[2,48,128]{2,1,0:T(8,128)(2,1)S(1)}, bf16[2,48,128]{2,1,0:T(8,128)(2,1)S(1)}, u32[]{:S(2)}, u32[]{:S(2)}) collective-permute-start(bf16[2,48,128]{2,1,0:T(8,128)(2,1)S(1)} %get-tuple-element.7), channel_id=1, source_target_pairs={{0,64},{64,0},{128,192},{192,128},{256,320},{320,256},{384,448},{4... | collective-permute-start | bytes 73736 | tf_op jit(solution)/shard_map/ppermute | solution.py:284
  87.1 0.8 collective-permute-done.8
  88.3 0.3 convolution_add_fusion
  88.5 0.2 slice.79
  88.8 0.2 slice.80
  89.1 0.2 slice.81
  89.4 0.2 slice.82
  89.7 0.2 slice.83
  89.9 0.2 slice.84
  90.2 0.1 slice.85
  90.3 0.1 copy.5
  90.5 0.7 fusion.1
  91.2 7.1 %all-to-all-done.1 = bf16[128,32,128]{2,1,0:T(8,128)(2,1)S(1)} async-done(((bf16[128,32,128]{2,1,0:T(8,128)(2,1)}), bf16[128,32,128]{2,1,0:T(8,128)(2,1)S(1)}, u32[]{:S(2)}, u32[]{:S(2)}) %all-to-all-start.1) | async-done | bytes 1048608 | tf_op jit(solution)/shard_map/all_to_all | solution.py:310
  98.4 1.1 %place.1 = bf16[128,4096]{1,0:T(8,128)(2,1)} custom-call(bf16[8,4,4,32,128]{4,3,2,1,0:T(8,128)(2,1)S(1)} %bitcast.39), custom_call_target="tpu_custom_call" | custom-call | tf_op jit(solution)/shard_map/place/pallas_call | solution.py:245
  (34 shorter events, 0.9 us)
Async XLA Ops:
  3.1 48.6 %all-to-all-start = ((bf16[64,32,128]{2,1,0:T(8,128)(2,1)}), bf16[64,32,128]{2,1,0:T(8,128)(2,1)S(1)}, u32[]{:S(2)}, u32[]{:S(2)}) async-start(bf16[64,32,128]{2,1,0:T(8,128)(2,1)} %bitcast.42), calls=%async_computation | async-start | bytes 1048576 | tf_op jit(solution)/shard_map/all_to_all | solution.py:306
  22.2 0.7 copy-start
  22.2 0.7 copy-start.1
  22.9 3.7 %collective-permute-start = (bf16[1,8,128]{2,1,0:T(8,128)(2,1)S(1)}, bf16[1,8,128]{2,1,0:T(8,128)(2,1)S(1)}, u32[]{:S(2)}, u32[]{:S(2)}) collective-permute-start(bf16[1,8,128]{2,1,0:T(8,128)(2,1)S(1)} %fusion.11), channel_id=1, source_target_pairs={{0,64},{64,0},{128,192},{192,128},{256,320},{320,256},{384,448},{4... | collective-permute-start | bytes 6152 | tf_op jit(solution)/shard_map/ppermute | solution.py:284
  26.5 9.7 %collective-permute-start.1 = (bf16[2,8,128]{2,1,0:T(8,128)(2,1)S(1)}, bf16[2,8,128]{2,1,0:T(8,128)(2,1)S(1)}, u32[]{:S(2)}, u32[]{:S(2)}) collective-permute-start(bf16[2,8,128]{2,1,0:T(8,128)(2,1)S(1)} %pad_maximum_fusion), channel_id=1, source_target_pairs={{0,128},{64,192},{128,0},{192,64},{256,384},{320,448},{384,256},{4... | collective-permute-start | bytes 12296 | tf_op jit(solution)/shard_map/ppermute | solution.py:299
  29.7 6.5 %collective-permute-start.2 = (bf16[2,8,128]{2,1,0:T(8,128)(2,1)S(1)}, bf16[2,8,128]{2,1,0:T(8,128)(2,1)S(1)}, u32[]{:S(2)}, u32[]{:S(2)}) collective-permute-start(bf16[2,8,128]{2,1,0:T(8,128)(2,1)S(1)} %pad_maximum_fusion), channel_id=1, source_target_pairs={{0,256},{64,320},{128,384},{192,448},{256,0},{320,64},{384,128},{4... | collective-permute-start | bytes 12296 | tf_op jit(solution)/shard_map/ppermute | solution.py:299
  34.3 5.9 %collective-permute-start.3 = (bf16[2,8,128]{2,1,0:T(8,128)(2,1)S(1)}, bf16[2,8,128]{2,1,0:T(8,128)(2,1)S(1)}, u32[]{:S(2)}, u32[]{:S(2)}) collective-permute-start(bf16[2,8,128]{2,1,0:T(8,128)(2,1)S(1)} %pad_maximum_fusion), channel_id=1, source_target_pairs={{0,384},{64,448},{128,256},{192,320},{256,128},{320,192},{384,0},{... | collective-permute-start | bytes 12296 | tf_op jit(solution)/shard_map/ppermute | solution.py:299
  40.1 0.7 collective-permute-start.4
  54.6 43.8 %all-to-all-start.1 = ((bf16[128,32,128]{2,1,0:T(8,128)(2,1)}), bf16[128,32,128]{2,1,0:T(8,128)(2,1)S(1)}, u32[]{:S(2)}, u32[]{:S(2)}) async-start(bf16[128,32,128]{2,1,0:T(8,128)(2,1)} %bitcast.6), calls=%async_computation.1 | async-start | bytes 2097152 | tf_op jit(solution)/shard_map/all_to_all | solution.py:310
  75.7 7.2 %collective-permute-start.5 = (bf16[2,2,48,128]{3,2,1,0:T(8,128)(2,1)S(1)}, bf16[2,2,48,128]{3,2,1,0:T(8,128)(2,1)S(1)}, u32[]{:S(2)}, u32[]{:S(2)}) collective-permute-start(bf16[2,2,48,128]{3,2,1,0:T(8,128)(2,1)S(1)} %get-tuple-element.2), channel_id=1, source_target_pairs={{0,128},{64,192},{132,4},{196,68},{264,392},{328,456},{396,268},{4... | collective-permute-start | bytes 147464 | tf_op jit(solution)/shard_map/ppermute | solution.py:280
  79.2 3.7 %collective-permute-start.6 = (bf16[2,2,48,128]{3,2,1,0:T(8,128)(2,1)S(1)}, bf16[2,2,48,128]{3,2,1,0:T(8,128)(2,1)S(1)}, u32[]{:S(2)}, u32[]{:S(2)}) collective-permute-start(bf16[2,2,48,128]{3,2,1,0:T(8,128)(2,1)S(1)} %get-tuple-element.4), channel_id=1, source_target_pairs={{0,256},{64,320},{132,388},{196,452},{264,8},{328,72},{396,140},{4... | collective-permute-start | bytes 147464 | tf_op jit(solution)/shard_map/ppermute | solution.py:280
  81.6 2.6 %collective-permute-start.7 = (bf16[2,2,48,128]{3,2,1,0:T(8,128)(2,1)S(1)}, bf16[2,2,48,128]{3,2,1,0:T(8,128)(2,1)S(1)}, u32[]{:S(2)}, u32[]{:S(2)}) collective-permute-start(bf16[2,2,48,128]{3,2,1,0:T(8,128)(2,1)S(1)} %get-tuple-element.3), channel_id=1, source_target_pairs={{0,384},{64,448},{132,260},{196,324},{264,136},{328,200},{396,12},... | collective-permute-start | bytes 147464 | tf_op jit(solution)/shard_map/ppermute | solution.py:280
  84.2 3.8 %collective-permute-start.8 = (bf16[2,48,128]{2,1,0:T(8,128)(2,1)S(1)}, bf16[2,48,128]{2,1,0:T(8,128)(2,1)S(1)}, u32[]{:S(2)}, u32[]{:S(2)}) collective-permute-start(bf16[2,48,128]{2,1,0:T(8,128)(2,1)S(1)} %get-tuple-element.7), channel_id=1, source_target_pairs={{0,64},{64,0},{128,192},{192,128},{256,320},{320,256},{384,448},{4... | collective-permute-start | bytes 73736 | tf_op jit(solution)/shard_map/ppermute | solution.py:284

commit v6 on v5

--- a/solution.py
+++ b/solution.py
@@ -105,8 +105,11 @@
         state[0, x] = x_ref[pl.ds(16 * x + SERVED * quarter - HALO, reach)]
 
     copies = []
+    ready = section_params(0, sec, quarter, par)
     for step in range(sections):
-        bands, gains = section_params(step, sec, quarter, par)
+        bands, gains = ready
+        if step + 1 < sections:
+            ready = section_params(step + 1, sec, quarter, par)
         count = reach - step
         for part in range(WIDE // GROUP):
             low = part * GROUP

time: 100 us -> 100 us (level)
  no operation moved by 1% of the time
where the time goes in v6:
time: 100 us; the launch traced here: 99.5 us
  starting transfers between devices  56.7 us (57%)
  waiting for transfers between devices  24.6 us (25%)
  Pallas kernels  13.2 us (13%)
  local copies, waits for them, and re-layouts  2.36 us (2%)
  other arithmetic  1.35 us (1%)
    all_to_all x1, starting transfers between devices, per_device(): lax.all_to_all(picked.reshape(64, WIDE, TAPS), ('x', 'quarter', 'slot'),...  19.1 us
    all_to_all x1, starting transfers between devices, per_device(): lax.all_to_all(outputs.reshape(sections * 16, WIDE, TAPS), ('section', 'x...  14.3 us
    all_to_all x1, waiting for transfers between devices, per_device(): lax.all_to_all(picked.reshape(64, WIDE, TAPS), ('x', 'quarter', 'slot'),...  10.8 us
    ppermute x3, starting transfers between devices, per_device(): lax.ppermute(params, 'section', [(i, i ^ 2 * offset) for i in range(8)])  9.64 us
    all_to_all x1, waiting for transfers between devices, per_device(): lax.all_to_all(outputs.reshape(sections * 16, WIDE, TAPS), ('section', 'x...  7.15 us
    ppermute x3, starting transfers between devices, home_round(): return lax.ppermute(value, EVERY, pairs)  7.14 us
    pallas_call x1, Pallas kernels, lag_info(): pl.pallas_call(lags_kernel, in_specs=[pl.BlockSpec(memory_space=pltpu.SME...  6.79 us
    ppermute x2, starting transfers between devices, swap_cores(): return lax.ppermute(value, 'section', [(i, i ^ 1) for i in range(8)])  5.79 us
  transfers between devices with their start and end apart: 11, of which 6 were waited for; matrix products, arithmetic and copies ran while one was open for 3% of the time, Pallas kernels for 7%

profile of v6, /device:TPU:1, one launch (start us, length us, event | category | flops | bytes accessed | tf_op | source)
XLA Modules:
  0.0 99.5 jit_solution(12669985445322889306)
XLA Ops:
  0.6 2.4 %pick.1 = bf16[16,128,128]{2,1,0:T(8,128)(2,1)} custom-call(s32[1]{0:T(128)} %bitcast.sec_ref, bf16[128,4096]{1,0:T(8,128)(2,1)} %slab_ref.1), custom_call_target="tpu_custom_call" | custom-call | tf_op jit(solution)/shard_map/pick/pallas_call | solution.py:54
  3.1 19.1 %all-to-all-start = ((bf16[64,32,128]{2,1,0:T(8,128)(2,1)}), bf16[64,32,128]{2,1,0:T(8,128)(2,1)S(1)}, u32[]{:S(2)}, u32[]{:S(2)}) async-start(bf16[64,32,128]{2,1,0:T(8,128)(2,1)} %bitcast.42), calls=%async_computation | async-start | bytes 1048576 | tf_op jit(solution)/shard_map/all_to_all | solution.py:309
  22.2 0.7 copy-done
  22.9 2.9 %collective-permute-start = (bf16[1,8,128]{2,1,0:T(8,128)(2,1)S(1)}, bf16[1,8,128]{2,1,0:T(8,128)(2,1)S(1)}, u32[]{:S(2)}, u32[]{:S(2)}) collective-permute-start(bf16[1,8,128]{2,1,0:T(8,128)(2,1)S(1)} %fusion.11), channel_id=1, source_target_pairs={{0,64},{64,0},{128,192},{192,128},{256,320},{320,256},{384,448},{4... | collective-permute-start | bytes 6152 | tf_op jit(solution)/shard_map/ppermute | solution.py:287
  25.8 0.8 collective-permute-done
  26.5 3.2 %collective-permute-start.1 = (bf16[2,8,128]{2,1,0:T(8,128)(2,1)S(1)}, bf16[2,8,128]{2,1,0:T(8,128)(2,1)S(1)}, u32[]{:S(2)}, u32[]{:S(2)}) collective-permute-start(bf16[2,8,128]{2,1,0:T(8,128)(2,1)S(1)} %pad_maximum_fusion), channel_id=1, source_target_pairs={{0,128},{64,192},{128,0},{192,64},{256,384},{320,448},{384,256},{4... | collective-permute-start | bytes 12296 | tf_op jit(solution)/shard_map/ppermute | solution.py:302
  29.7 4.5 %collective-permute-start.2 = (bf16[2,8,128]{2,1,0:T(8,128)(2,1)S(1)}, bf16[2,8,128]{2,1,0:T(8,128)(2,1)S(1)}, u32[]{:S(2)}, u32[]{:S(2)}) collective-permute-start(bf16[2,8,128]{2,1,0:T(8,128)(2,1)S(1)} %pad_maximum_fusion), channel_id=1, source_target_pairs={{0,256},{64,320},{128,384},{192,448},{256,0},{320,64},{384,128},{4... | collective-permute-start | bytes 12296 | tf_op jit(solution)/shard_map/ppermute | solution.py:302
  34.3 1.9 %collective-permute-start.3 = (bf16[2,8,128]{2,1,0:T(8,128)(2,1)S(1)}, bf16[2,8,128]{2,1,0:T(8,128)(2,1)S(1)}, u32[]{:S(2)}, u32[]{:S(2)}) collective-permute-start(bf16[2,8,128]{2,1,0:T(8,128)(2,1)S(1)} %pad_maximum_fusion), channel_id=1, source_target_pairs={{0,384},{64,448},{128,256},{192,320},{256,128},{320,192},{384,0},{... | collective-permute-start | bytes 12296 | tf_op jit(solution)/shard_map/ppermute | solution.py:302
  36.3 3.9 %collective-permute-done.3 = bf16[2,8,128]{2,1,0:T(8,128)(2,1)S(1)} collective-permute-done((bf16[2,8,128]{2,1,0:T(8,128)(2,1)S(1)}, bf16[2,8,128]{2,1,0:T(8,128)(2,1)S(1)}, u32[]{:S(2)}, u32[]{:S(2)}) %collective-permute-start.3) | collective-permute-done | bytes 4128 | tf_op jit(solution)/shard_map/ppermute | solution.py:302
  40.1 0.7 collective-permute-start.4
  40.9 10.8 %all-to-all-done.x_ref = bf16[64,32,128]{2,1,0:T(8,128)(2,1)S(1)} async-done(((bf16[64,32,128]{2,1,0:T(8,128)(2,1)}), bf16[64,32,128]{2,1,0:T(8,128)(2,1)S(1)}, u32[]{:S(2)}, u32[]{:S(2)}) %all-to-all-start) | async-done | bytes 524320 | tf_op jit(solution)/shard_map/all_to_all | solution.py:309
  51.7 2.9 %serve.1 = bf16[8,4,4,32,128]{4,3,2,1,0:T(8,128)(2,1)} custom-call(s32[2]{0:T(128)S(1)} %pad_add_fusion.7.where_ref, bf16[64,32,128]{2,1,0:T(8,128)(2,1)S(1)} %all-to-all-done.x_ref, bf16[64,128]{1,0:T(8,128)(2,1)S(1)} %bitcast.40), custom_call_target="tpu_custom_call" | custom-call | tf_op jit(solution)/shard_map/serve/pallas_call | solution.py:134
  54.6 14.3 %all-to-all-start.1 = ((bf16[128,32,128]{2,1,0:T(8,128)(2,1)}), bf16[128,32,128]{2,1,0:T(8,128)(2,1)S(1)}, u32[]{:S(2)}, u32[]{:S(2)}) async-start(bf16[128,32,128]{2,1,0:T(8,128)(2,1)} %bitcast.6), calls=%async_computation.1 | async-start | bytes 2097152 | tf_op jit(solution)/shard_map/all_to_all | solution.py:313
  68.9 6.8 %lags.1 = bf16[4,2,2,48,128]{4,3,2,1,0:T(8,128)(2,1)S(1)} custom-call(s32[2]{0:T(128)S(1)} %pad_add_fusion.7.where_ref, bf16[64,32,128]{2,1,0:T(8,128)(2,1)S(1)} %all-to-all-done.x_ref, bf16[64,128]{1,0:T(8,128)(2,1)S(1)} %bitcast.41), custom_call_target="tpu_custom_call" | custom-call | flops 2147483648 | bytes 8388608 | tf_op jit(solution)/shard_map/lags/pallas_call | solution.py:207
  75.7 3.5 %collective-permute-start.5 = (bf16[2,2,48,128]{3,2,1,0:T(8,128)(2,1)S(1)}, bf16[2,2,48,128]{3,2,1,0:T(8,128)(2,1)S(1)}, u32[]{:S(2)}, u32[]{:S(2)}) collective-permute-start(bf16[2,2,48,128]{3,2,1,0:T(8,128)(2,1)S(1)} %get-tuple-element.2), channel_id=1, source_target_pairs={{0,128},{64,192},{132,4},{196,68},{264,392},{328,456},{396,268},{4... | collective-permute-start | bytes 147464 | tf_op jit(solution)/shard_map/ppermute | solution.py:283
  79.2 2.4 %collective-permute-start.6 = (bf16[2,2,48,128]{3,2,1,0:T(8,128)(2,1)S(1)}, bf16[2,2,48,128]{3,2,1,0:T(8,128)(2,1)S(1)}, u32[]{:S(2)}, u32[]{:S(2)}) collective-permute-start(bf16[2,2,48,128]{3,2,1,0:T(8,128)(2,1)S(1)} %get-tuple-element.4), channel_id=1, source_target_pairs={{0,256},{64,320},{132,388},{196,452},{264,8},{328,72},{396,140},{4... | collective-permute-start | bytes 147464 | tf_op jit(solution)/shard_map/ppermute | solution.py:283
  81.6 1.3 %collective-permute-start.7 = (bf16[2,2,48,128]{3,2,1,0:T(8,128)(2,1)S(1)}, bf16[2,2,48,128]{3,2,1,0:T(8,128)(2,1)S(1)}, u32[]{:S(2)}, u32[]{:S(2)}) collective-permute-start(bf16[2,2,48,128]{3,2,1,0:T(8,128)(2,1)S(1)} %get-tuple-element.3), channel_id=1, source_target_pairs={{0,384},{64,448},{132,260},{196,324},{264,136},{328,200},{396,12},... | collective-permute-start | bytes 147464 | tf_op jit(solution)/shard_map/ppermute | solution.py:283
  82.9 1.2 %collective-permute-done.7 = bf16[2,2,48,128]{3,2,1,0:T(8,128)(2,1)S(1)} collective-permute-done((bf16[2,2,48,128]{3,2,1,0:T(8,128)(2,1)S(1)}, bf16[2,2,48,128]{3,2,1,0:T(8,128)(2,1)S(1)}, u32[]{:S(2)}, u32[]{:S(2)}) %collective-permute-start.7) | collective-permute-done | bytes 49184 | tf_op jit(solution)/shard_map/ppermute | solution.py:283
  84.2 2.9 %collective-permute-start.8 = (bf16[2,48,128]{2,1,0:T(8,128)(2,1)S(1)}, bf16[2,48,128]{2,1,0:T(8,128)(2,1)S(1)}, u32[]{:S(2)}, u32[]{:S(2)}) collective-permute-start(bf16[2,48,128]{2,1,0:T(8,128)(2,1)S(1)} %get-tuple-element.7), channel_id=1, source_target_pairs={{0,64},{64,0},{128,192},{192,128},{256,320},{320,256},{384,448},{4... | collective-permute-start | bytes 73736 | tf_op jit(solution)/shard_map/ppermute | solution.py:287
  87.1 0.8 collective-permute-done.8
  88.3 0.3 convolution_add_fusion
  88.5 0.2 slice.79
  88.8 0.2 slice.80
  89.1 0.2 slice.81
  89.4 0.2 slice.82
  89.7 0.2 slice.83
  89.9 0.2 slice.84
  90.2 0.1 slice.85
  90.3 0.1 copy.5
  90.5 0.7 fusion.1
  91.2 7.1 %all-to-all-done.1 = bf16[128,32,128]{2,1,0:T(8,128)(2,1)S(1)} async-done(((bf16[128,32,128]{2,1,0:T(8,128)(2,1)}), bf16[128,32,128]{2,1,0:T(8,128)(2,1)S(1)}, u32[]{:S(2)}, u32[]{:S(2)}) %all-to-all-start.1) | async-done | bytes 1048608 | tf_op jit(solution)/shard_map/all_to_all | solution.py:313
  98.4 1.1 %place.1 = bf16[128,4096]{1,0:T(8,128)(2,1)} custom-call(bf16[8,4,4,32,128]{4,3,2,1,0:T(8,128)(2,1)S(1)} %bitcast.39), custom_call_target="tpu_custom_call" | custom-call | tf_op jit(solution)/shard_map/place/pallas_call | solution.py:248
  (34 shorter events, 0.9 us)
Async XLA Ops:
  3.1 48.6 %all-to-all-start = ((bf16[64,32,128]{2,1,0:T(8,128)(2,1)}), bf16[64,32,128]{2,1,0:T(8,128)(2,1)S(1)}, u32[]{:S(2)}, u32[]{:S(2)}) async-start(bf16[64,32,128]{2,1,0:T(8,128)(2,1)} %bitcast.42), calls=%async_computation | async-start | bytes 1048576 | tf_op jit(solution)/shard_map/all_to_all | solution.py:309
  22.2 0.7 copy-start
  22.2 0.7 copy-start.1
  22.9 3.7 %collective-permute-start = (bf16[1,8,128]{2,1,0:T(8,128)(2,1)S(1)}, bf16[1,8,128]{2,1,0:T(8,128)(2,1)S(1)}, u32[]{:S(2)}, u32[]{:S(2)}) collective-permute-start(bf16[1,8,128]{2,1,0:T(8,128)(2,1)S(1)} %fusion.11), channel_id=1, source_target_pairs={{0,64},{64,0},{128,192},{192,128},{256,320},{320,256},{384,448},{4... | collective-permute-start | bytes 6152 | tf_op jit(solution)/shard_map/ppermute | solution.py:287
  26.5 9.7 %collective-permute-start.1 = (bf16[2,8,128]{2,1,0:T(8,128)(2,1)S(1)}, bf16[2,8,128]{2,1,0:T(8,128)(2,1)S(1)}, u32[]{:S(2)}, u32[]{:S(2)}) collective-permute-start(bf16[2,8,128]{2,1,0:T(8,128)(2,1)S(1)} %pad_maximum_fusion), channel_id=1, source_target_pairs={{0,128},{64,192},{128,0},{192,64},{256,384},{320,448},{384,256},{4... | collective-permute-start | bytes 12296 | tf_op jit(solution)/shard_map/ppermute | solution.py:302
  29.7 6.5 %collective-permute-start.2 = (bf16[2,8,128]{2,1,0:T(8,128)(2,1)S(1)}, bf16[2,8,128]{2,1,0:T(8,128)(2,1)S(1)}, u32[]{:S(2)}, u32[]{:S(2)}) collective-permute-start(bf16[2,8,128]{2,1,0:T(8,128)(2,1)S(1)} %pad_maximum_fusion), channel_id=1, source_target_pairs={{0,256},{64,320},{128,384},{192,448},{256,0},{320,64},{384,128},{4... | collective-permute-start | bytes 12296 | tf_op jit(solution)/shard_map/ppermute | solution.py:302
  34.3 5.9 %collective-permute-start.3 = (bf16[2,8,128]{2,1,0:T(8,128)(2,1)S(1)}, bf16[2,8,128]{2,1,0:T(8,128)(2,1)S(1)}, u32[]{:S(2)}, u32[]{:S(2)}) collective-permute-start(bf16[2,8,128]{2,1,0:T(8,128)(2,1)S(1)} %pad_maximum_fusion), channel_id=1, source_target_pairs={{0,384},{64,448},{128,256},{192,320},{256,128},{320,192},{384,0},{... | collective-permute-start | bytes 12296 | tf_op jit(solution)/shard_map/ppermute | solution.py:302
  40.1 0.7 collective-permute-start.4
  54.6 43.8 %all-to-all-start.1 = ((bf16[128,32,128]{2,1,0:T(8,128)(2,1)}), bf16[128,32,128]{2,1,0:T(8,128)(2,1)S(1)}, u32[]{:S(2)}, u32[]{:S(2)}) async-start(bf16[128,32,128]{2,1,0:T(8,128)(2,1)} %bitcast.6), calls=%async_computation.1 | async-start | bytes 2097152 | tf_op jit(solution)/shard_map/all_to_all | solution.py:313
  75.7 7.2 %collective-permute-start.5 = (bf16[2,2,48,128]{3,2,1,0:T(8,128)(2,1)S(1)}, bf16[2,2,48,128]{3,2,1,0:T(8,128)(2,1)S(1)}, u32[]{:S(2)}, u32[]{:S(2)}) collective-permute-start(bf16[2,2,48,128]{3,2,1,0:T(8,128)(2,1)S(1)} %get-tuple-element.2), channel_id=1, source_target_pairs={{0,128},{64,192},{132,4},{196,68},{264,392},{328,456},{396,268},{4... | collective-permute-start | bytes 147464 | tf_op jit(solution)/shard_map/ppermute | solution.py:283
  79.2 3.7 %collective-permute-start.6 = (bf16[2,2,48,128]{3,2,1,0:T(8,128)(2,1)S(1)}, bf16[2,2,48,128]{3,2,1,0:T(8,128)(2,1)S(1)}, u32[]{:S(2)}, u32[]{:S(2)}) collective-permute-start(bf16[2,2,48,128]{3,2,1,0:T(8,128)(2,1)S(1)} %get-tuple-element.4), channel_id=1, source_target_pairs={{0,256},{64,320},{132,388},{196,452},{264,8},{328,72},{396,140},{4... | collective-permute-start | bytes 147464 | tf_op jit(solution)/shard_map/ppermute | solution.py:283
  81.6 2.6 %collective-permute-start.7 = (bf16[2,2,48,128]{3,2,1,0:T(8,128)(2,1)S(1)}, bf16[2,2,48,128]{3,2,1,0:T(8,128)(2,1)S(1)}, u32[]{:S(2)}, u32[]{:S(2)}) collective-permute-start(bf16[2,2,48,128]{3,2,1,0:T(8,128)(2,1)S(1)} %get-tuple-element.3), channel_id=1, source_target_pairs={{0,384},{64,448},{132,260},{196,324},{264,136},{328,200},{396,12},... | collective-permute-start | bytes 147464 | tf_op jit(solution)/shard_map/ppermute | solution.py:283
  84.2 3.8 %collective-permute-start.8 = (bf16[2,48,128]{2,1,0:T(8,128)(2,1)S(1)}, bf16[2,48,128]{2,1,0:T(8,128)(2,1)S(1)}, u32[]{:S(2)}, u32[]{:S(2)}) collective-permute-start(bf16[2,48,128]{2,1,0:T(8,128)(2,1)S(1)} %get-tuple-element.7), channel_id=1, source_target_pairs={{0,64},{64,0},{128,192},{192,128},{256,320},{320,256},{384,448},{4... | collective-permute-start | bytes 73736 | tf_op jit(solution)/shard_map/ppermute | solution.py:287
